TPU v7x, 32 devices: a whole 2x2x4 slice. The times are simulated.
32 devices in a mesh: tiles: 2 (over x), disp: 8 (over z, y), rows: 2 (over core).
Axes of the slice: x: 2, y: 2, z: 4, core: 2. Of those that a mesh axis runs over, the one named last changes fastest.
Arguments:
- volume: bfloat16 [32, 192, 64, 512], P(None, 'disp', ('tiles', 'rows')), parts along dimension 2, may hold values from -1000 to 1000, as said below
- conv_weight: bfloat16 [27, 32, 32], replicated, may hold values from -0.21875 to 0.21875
- conv_bias: float32 [32], replicated, may hold values from -3 to 3
- reg_weight: bfloat16 [27, 32], replicated, may hold values from -0.875 to 0.875
Outputs:
- disparity: float32 [64, 512], P(('tiles', 'rows')), parts along dimension 0
There are 2 independent parts, one for each index of `tiles`. A program takes and returns all parts, laid end to end along the dimension named above; an argument that names none is the same for every part. Nothing has to cross between parts.
Inputs may be any that keep to these rules, and one draw needn't show every extreme that they name: `volume`: Real-valued matching features.
All inputs are finite; a program needn't handle non-finite values.
Results may differ from a plain program's by a relative error of at most 0.008.
Values may be sent and summed in bfloat16 or wider, within the bound.
A program may use at most 384 MiB of HBM per device.

v0:
```python
import jax
import jax.numpy as jnp
from jax import lax
from jax.sharding import PartitionSpec as P


def padded(x, sides, width):
    for axis, dim in sides:
        count, length = (lax.axis_size(axis), x.shape[dim])
        up = [(i, (i + 1) % count) for i in range(count - 1)]
        down = [(j, i) for i, j in up]
        last = lax.slice_in_dim(x, length - width, length, axis=dim)
        initial = lax.slice_in_dim(x, 0, width, axis=dim)
        before = lax.ppermute(last, axis, up)
        after = lax.ppermute(initial, axis, down)
        x = jnp.concatenate([before, x, after], axis=dim)
    return x


def joined(value, axis, join):
    pieces = jax.tree.map(lambda part: lax.all_gather(part, axis), value)
    head = jax.tree.map(lambda part: part[0], pieces)
    tail = jax.tree.map(lambda part: part[1:], pieces)
    running, _ = lax.scan(lambda running, slab: (join(running, slab), None), head, tail)
    return running


def aggregate(extended, conv_weight):
    out_depth = extended.shape[1] - 2
    out_rows = extended.shape[2] - 2
    out_cols = extended.shape[3] - 2
    stacked = jnp.stack(
        [extended[:, :, :, col_tap : col_tap + out_cols] for col_tap in range(3)], 0
    )
    summed = None
    for depth_tap in range(3):
        for row_tap in range(3):
            start = 9 * depth_tap + 3 * row_tap
            kernel = conv_weight[start : start + 3]
            window = stacked[
                :, :, depth_tap : depth_tap + out_depth, row_tap : row_tap + out_rows, :
            ]
            term = jnp.einsum("koc,kcdhw->odhw", kernel, window, preferred_element_type=jnp.float32)
            summed = term if summed is None else summed + term
    return summed


def regress(extended, reg_weight):
    depth = extended.shape[1] - 2
    height = extended.shape[2] - 2
    width = extended.shape[3] - 2
    tapped = jnp.einsum("tc,cdhw->tdhw", reg_weight, extended, preferred_element_type=jnp.float32)
    cost = None
    for depth_tap in range(3):
        for row_tap in range(3):
            for col_tap in range(3):
                piece = tapped[
                    9 * depth_tap + 3 * row_tap + col_tap,
                    depth_tap : depth_tap + depth,
                    row_tap : row_tap + height,
                    col_tap : col_tap + width,
                ]
                cost = piece if cost is None else cost + piece
    return cost


def pad_columns(array):
    return jnp.pad(array, ((0, 0), (0, 0), (0, 0), (1, 1)))


def combine(first, second):
    peak = jnp.maximum(first[0], second[0])
    left = jnp.exp(first[0] - peak)
    right = jnp.exp(second[0] - peak)
    return (peak, first[1] * left + second[1] * right, first[2] * left + second[2] * right)


def body(volume, conv_weight, conv_bias, reg_weight):
    planes_dev = volume.shape[1]
    bias = conv_bias[:, None, None, None]
    extended = padded(volume, (("disp", 1), ("rows", 2)), 1)
    summed = aggregate(pad_columns(extended), conv_weight)
    hidden = jnp.maximum(summed + bias, 0.0).astype(jnp.bfloat16)
    hidden_ext = padded(hidden, (("disp", 1), ("rows", 2)), 1)
    cost = regress(pad_columns(hidden_ext), reg_weight)
    score = -cost
    local_peak = jnp.max(score, axis=0)
    expo = jnp.exp(score - local_peak[None])
    planes = (lax.axis_index("disp") * planes_dev + jnp.arange(planes_dev, dtype=jnp.int32)).astype(
        jnp.float32
    )
    total = jnp.sum(expo, axis=0)
    moment = jnp.sum(planes[:, None, None] * expo, axis=0)
    peak, total, moment = joined((local_peak, total, moment), "disp", combine)
    return moment / total


def solution(mesh):
    in_specs = (P(None, "disp", ("tiles", "rows"), None), P(), P(), P())
    out_specs = P(("tiles", "rows"), None)
    return jax.shard_map(body, mesh=mesh, in_specs=in_specs, out_specs=out_specs, check_vma=False)
```

profile of v0, /device:TPU:0, one launch (start us, length us, event | category | flops | bytes accessed | tf_op | source)
XLA Modules:
  0.0 613.3 jit_solution(1206597589906461967)
XLA Ops:
  1.6 4.9 collective-permute-start
  8.1 20.8 %collective-permute-done = bf16[32,1,16,512]{3,0,2,1:T(8,128)(2,1)S(1)} collective-permute-done((bf16[32,1,16,512]{3,0,2,1:T(8,128)(2,1)S(1)}, bf16[32,1,16,512]{3,0,2,1:T(8,128)(2,1)S(1)}, u32[]{:S(2)}, u32[]{:S(2)}) %collective-permute-start) | collective-permute-done | bytes 524320 | tf_op jit(solution)/shard_map/ppermute | solution.py:14
  28.9 12.9 %constant_dynamic-update-slice_fusion.1 = bf16[32,26,16,512]{3,0,2,1:T(8,128)(2,1)S(1)} fusion(bf16[32,26,16,512]{3,0,2,1:T(8,128)(2,1)S(1)} %constant_dynamic-update-slice_fusion.2, bf16[32,24,16,512]{3,2,1,0:T(8,128)(2,1)} %param.6), kind=kLoop, calls=%fused_computation.124 | loop fusion | bytes 25165824
  47.6 7.0 %fusion.83 = (bf16[1,32,26,18,512]{4,1,0,3,2:T(8,128)(2,1)}, bf16[32,26,18,512]{3,0,2,1:T(8,128)(2,1)S(1)}) fusion(bf16[32,26,1,512]{3,0,2,1:T(8,128)(2,1)S(1)} %collective-permute-done.3, bf16[32,26,16,512]{3,0,2,1:T(8,128)(2,1)S(1)} %constant_dynamic-update-slice_fusion, bf16[32,26,1,512]{3,0,2,1:T(8,128)(2,1)S(1)} %collective-permute-done.2), kind=kLoop, calls=%fused_computation.132 | loop fusion | flops 15335424 | bytes 46006272 | tf_op jit(solution)/shard_map/stack | solution.py:32
  54.6 18.4 %fusion.41 = (bf16[1,32,26,18,512]{4,1,0,3,2:T(8,128)(2,1)}, bf16[1,32,26,18,512]{4,1,0,3,2:T(8,128)(2,1)}) fusion(bf16[32,26,18,512]{3,0,2,1:T(8,128)(2,1)S(1)} %get-tuple-element.95), kind=kLoop, calls=%fused_computation.57 | loop fusion | bytes 46006272 | tf_op jit(solution)/shard_map/stack | solution.py:32
  73.1 30.5 %pad_maximum_fusion = bf16[3,32,26,18,512]{4,1,0,3,2:T(8,128)(2,1)} fusion(bf16[1,32,26,18,512]{4,1,0,3,2:T(8,128)(2,1)} %get-tuple-element.93, bf16[1,32,26,18,512]{4,1,0,3,2:T(8,128)(2,1)} %get-tuple-element.94, bf16[1,32,26,18,512]{4,1,0,3,2:T(8,128)(2,1)} %get-tuple-element.92), kind=kLoop, calls=%fused_computation.10 | loop fusion | flops 46006272 | bytes 92012544 | tf_op jit(solution)/shard_map/stack | solution.py:32
  103.6 23.2 %fusion.10 = f32[24,16,512,32,1]{2,3,4,1,0:T(8,128)} fusion(bf16[3,32,26,18,512]{4,1,0,3,2:T(8,128)(2,1)} %pad_maximum_fusion, bf16[27,32,32]{2,1,0:T(8,128)(2,1)S(1)} %copy-done.1), kind=kOutput, calls=%fused_computation.18 | convolution fusion | flops 1207959552 | bytes 62939136 | tf_op jit(solution)/shard_map/koc,kcdhw->odhw/dot_general | solution.py:43
  126.8 23.2 %fusion.12 = f32[24,16,512,32,1]{2,3,4,1,0:T(8,128)} fusion(bf16[3,32,26,18,512]{4,1,0,3,2:T(8,128)(2,1)} %pad_maximum_fusion, bf16[27,32,32]{2,1,0:T(8,128)(2,1)S(1)} %copy-done.1), kind=kOutput, calls=%fused_computation.20 | convolution fusion | flops 1207959552 | bytes 62939136 | tf_op jit(solution)/shard_map/koc,kcdhw->odhw/dot_general | solution.py:43
  150.0 23.3 %fusion.14 = f32[24,16,512,32,1]{2,3,4,1,0:T(8,128)} fusion(bf16[3,32,26,18,512]{4,1,0,3,2:T(8,128)(2,1)} %pad_maximum_fusion, bf16[27,32,32]{2,1,0:T(8,128)(2,1)S(1)} %copy-done.1), kind=kOutput, calls=%fused_computation.22 | convolution fusion | flops 1207959552 | bytes 62939136 | tf_op jit(solution)/shard_map/koc,kcdhw->odhw/dot_general | solution.py:43
  173.3 23.2 %fusion.16 = f32[24,16,512,32,1]{2,3,4,1,0:T(8,128)} fusion(bf16[3,32,26,18,512]{4,1,0,3,2:T(8,128)(2,1)} %pad_maximum_fusion, bf16[27,32,32]{2,1,0:T(8,128)(2,1)S(1)} %copy-done.1), kind=kOutput, calls=%fused_computation.24 | convolution fusion | flops 1207959552 | bytes 62939136 | tf_op jit(solution)/shard_map/koc,kcdhw->odhw/dot_general | solution.py:43
  196.4 23.2 %fusion.18 = f32[24,16,512,32,1]{2,3,4,1,0:T(8,128)} fusion(bf16[3,32,26,18,512]{4,1,0,3,2:T(8,128)(2,1)} %pad_maximum_fusion, bf16[27,32,32]{2,1,0:T(8,128)(2,1)S(1)} %copy-done.1), kind=kOutput, calls=%fused_computation.26 | convolution fusion | flops 1207959552 | bytes 62939136 | tf_op jit(solution)/shard_map/koc,kcdhw->odhw/dot_general | solution.py:43
  219.6 23.4 %fusion.20 = f32[24,16,512,32,1]{2,3,4,1,0:T(8,128)} fusion(bf16[3,32,26,18,512]{4,1,0,3,2:T(8,128)(2,1)} %pad_maximum_fusion, bf16[27,32,32]{2,1,0:T(8,128)(2,1)S(1)} %copy-done.1), kind=kOutput, calls=%fused_computation.28 | convolution fusion | flops 1207959552 | bytes 62939136 | tf_op jit(solution)/shard_map/koc,kcdhw->odhw/dot_general | solution.py:43
  243.0 23.2 %fusion.6 = f32[24,16,512,32,1]{2,3,4,1,0:T(8,128)} fusion(bf16[3,32,26,18,512]{4,1,0,3,2:T(8,128)(2,1)} %pad_maximum_fusion, bf16[27,32,32]{2,1,0:T(8,128)(2,1)S(1)} %copy-done.1), kind=kOutput, calls=%fused_computation.14 | convolution fusion | flops 1207959552 | bytes 62939136 | tf_op jit(solution)/shard_map/koc,kcdhw->odhw/dot_general | solution.py:43
  266.2 23.2 %fusion.8 = f32[24,16,512,32,1]{2,3,4,1,0:T(8,128)} fusion(bf16[3,32,26,18,512]{4,1,0,3,2:T(8,128)(2,1)} %pad_maximum_fusion, bf16[27,32,32]{2,1,0:T(8,128)(2,1)S(1)} %copy-done.1), kind=kOutput, calls=%fused_computation.16 | convolution fusion | flops 1207959552 | bytes 62939136 | tf_op jit(solution)/shard_map/koc,kcdhw->odhw/dot_general | solution.py:43
  289.4 77.6 %fusion.43 = bf16[32,24,16,512]{3,0,2,1:T(8,128)(2,1)} fusion(f32[32]{0:T(128)S(1)} %copy-done.2, f32[24,16,512,32,1]{2,3,4,1,0:T(8,128)} %fusion.6, f32[24,16,512,32,1]{2,3,4,1,0:T(8,128)} %fusion.8, f32[24,16,512,32,1]{2,3,4,1,0:T(8,128)} %fusion.10, f32[24,16,512,32,1]{2,3,4,1,0:T(8,128)} %fusion.12, f32[24,16,512,32,1]{2,3,4,1,0:T(8,128)} %fusion.14, ...), kind=kOutput, calls=%fused_computation.60 | convolution fusion | flops 1277165568 | bytes 251683328 | tf_op jit(solution)/shard_map/koc,kcdhw->odhw/dot_general | solution.py:43
  368.2 4.4 collective-permute-start.4
  373.9 21.4 %collective-permute-done.4 = bf16[32,1,16,512]{3,0,2,1:T(8,128)(2,1)S(1)} collective-permute-done((bf16[32,1,16,512]{3,0,2,1:T(8,128)(2,1)S(1)}, bf16[32,1,16,512]{3,0,2,1:T(8,128)(2,1)S(1)}, u32[]{:S(2)}, u32[]{:S(2)}) %collective-permute-start.4) | collective-permute-done | bytes 524320 | tf_op jit(solution)/shard_map/ppermute | solution.py:14
  403.5 27.8 %fusion.40 = f32[27,26,18,514]{3,0,2,1:T(8,128)} fusion(bf16[32,26,1,512]{3,0,2,1:T(8,128)(2,1)} %collective-permute-done.7, bf16[32,26,1,512]{3,0,2,1:T(8,128)(2,1)} %collective-permute-done.6, bf16[32,1,16,512]{3,0,2,1:T(8,128)(2,1)S(1)} %collective-permute-done.5, bf16[32,24,16,512]{3,0,2,1:T(8,128)(2,1)} %fusion.43, ...), kind=kOutput, calls=%fused_computation.56 | convolution fusion | flops 554231808 | bytes 41316768 | tf_op jit(solution)/shard_map/tc,cdhw->tdhw/dot_general | solution.py:52
  431.3 24.7 %fusion.87 = (f32[1,24,16,512]{3,0,2,1:T(1,128)S(1)}, f32[1,24,16,512]{3,0,2,1:T(1,128)S(1)}, f32[1,24,16,512]{3,0,2,1:T(1,128)}, f32[1,24,16,512]{3,0,2,1:T(1,1...) fusion(f32[27,26,18,514]{3,0,2,1:T(8,128)} %fusion.40), kind=kLoop, calls=%fused_computation.135 | loop fusion | bytes 12582912 | tf_op jit(solution)/shard_map/slice | solution.py:57
  456.0 53.0 %fusion.86 = (f32[1,24,16,512]{3,0,2,1:T(1,128)}, f32[1,24,16,512]{3,0,2,1:T(1,128)}, f32[1,24,16,512]{3,0,2,1:T(1,128)}, f32[1,24,16,512]{3,0,2,1:T(1,128)}, f3...) fusion(f32[27,26,18,514]{3,0,2,1:T(8,128)} %fusion.40), kind=kLoop, calls=%fused_computation.134 | loop fusion | bytes 29884416 | tf_op jit(solution)/shard_map/slice | solution.py:57
  509.3 9.9 %fusion.84 = (f32[16,512]{1,0:T(8,128)S(1)}, f32[24,16,512]{2,1,0:T(8,128)S(1)}) fusion(f32[1,24,16,512]{3,2,0,1:T(8,128)S(1)} %copy.55, f32[1,24,16,512]{3,0,2,1:T(1,128)} %get-tuple-element.91, f32[1,24,16,512]{3,0,2,1:T(1,128)} %get-tuple-element.66, f32[1,24,16,512]{3,0,2,1:T(1,128)} %get-tuple-element.67, f32[1,24,16,512]{3,0,2,1:T(1,128)} %get-tuple-element.68, ...), kind=kLoop, calls=%fused_computation.133 | loop fusion | flops 5300224 | bytes 21266432 | tf_op jit(solution)/shard_map/reduce_max | solution.py:87
  519.4 30.8 %all-gather.1 = f32[128,512]{1,0:T(8,128)S(1)} all-gather(f32[16,512]{1,0:T(8,128)S(1)} %get-tuple-element.46), channel_id=3, replica_groups=mesh['tiles'=2,'disp'=8,'rows'=2] {'disp'}, dimensions={0}, use_global_device_ids=true | all-gather | bytes 294912 | tf_op jit(solution)/shard_map/all_gather | solution.py:21
  550.2 30.7 %all-gather.2 = f32[128,512]{1,0:T(8,128)S(1)} all-gather(f32[16,512]{1,0:T(8,128)S(1)} %get-tuple-element.45), channel_id=4, replica_groups=mesh['tiles'=2,'disp'=8,'rows'=2] {'disp'}, dimensions={0}, use_global_device_ids=true | all-gather | bytes 294912 | tf_op jit(solution)/shard_map/all_gather | solution.py:21
  581.0 30.7 %all-gather = f32[128,512]{1,0:T(8,128)S(1)} all-gather(f32[16,512]{1,0:T(8,128)S(1)} %get-tuple-element.63), channel_id=2, replica_groups=mesh['tiles'=2,'disp'=8,'rows'=2] {'disp'}, dimensions={0}, use_global_device_ids=true | all-gather | bytes 294912 | tf_op jit(solution)/shard_map/all_gather | solution.py:21
  (59 shorter events, 22.0 us)
Async XLA Ops:
  0.0 403.5 %copy-start = (bf16[27,32]{1,0:T(8,128)(2,1)S(1)}, bf16[27,32]{1,0:T(8,128)(2,1)}, u32[]{:S(2)}) copy-start(bf16[27,32]{1,0:T(8,128)(2,1)} %param.9) | copy-start | bytes 5188
  1.6 27.3 %collective-permute-start = (bf16[32,1,16,512]{3,0,2,1:T(8,128)(2,1)S(1)}, bf16[32,1,16,512]{3,0,2,1:T(8,128)(2,1)S(1)}, u32[]{:S(2)}, u32[]{:S(2)}) collective-permute-start(bf16[32,1,16,512]{3,0,2,1:T(8,128)(2,1)S(1)} %copy.179), channel_id=1, source_target_pairs={{0,2},{2,4},{4,6},{6,8},{8,10},{10,12},{12,14},{1,3},{3,5},{5,7},{... | collective-permute-start | bytes 1572872 | tf_op jit(solution)/shard_map/ppermute | solution.py:14
  6.8 35.0 %collective-permute-start.1 = (bf16[32,1,16,512]{3,0,2,1:T(8,128)(2,1)S(1)}, bf16[32,1,16,512]{3,0,2,1:T(8,128)(2,1)S(1)}, u32[]{:S(2)}, u32[]{:S(2)}) collective-permute-start(bf16[32,1,16,512]{3,0,2,1:T(8,128)(2,1)S(1)} %copy.180), channel_id=1, source_target_pairs={{2,0},{4,2},{6,4},{8,6},{10,8},{12,10},{14,12},{3,1},{5,3},{7,5},{... | collective-permute-start | bytes 1572872 | tf_op jit(solution)/shard_map/ppermute | solution.py:15
  42.0 3.3 collective-permute-start.2
  43.3 4.3 collective-permute-start.3
  73.1 30.5 %copy-start.1 = (bf16[27,32,32]{2,1,0:T(8,128)(2,1)S(1)}, bf16[27,32,32]{2,1,0:T(8,128)(2,1)}, u32[]{:S(2)}) copy-start(bf16[27,32,32]{2,1,0:T(8,128)(2,1)} %param.7) | copy-start | bytes 165892
  266.2 23.2 %copy-start.2 = (f32[32]{0:T(128)S(1)}, f32[32]{0:T(128)}, u32[]{:S(2)}) copy-start(f32[32]{0:T(128)} %param.8) | copy-start | bytes 388
  368.2 27.1 %collective-permute-start.4 = (bf16[32,1,16,512]{3,0,2,1:T(8,128)(2,1)S(1)}, bf16[32,1,16,512]{3,0,2,1:T(8,128)(2,1)S(1)}, u32[]{:S(2)}, u32[]{:S(2)}) collective-permute-start(bf16[32,1,16,512]{3,0,2,1:T(8,128)(2,1)S(1)} %get-tuple-element.100), channel_id=1, source_target_pairs={{0,2},{2,4},{4,6},{6,8},{8,10},{10,12},{12,14},{1,3},{3,5},{5,7},{... | collective-permute-start | bytes 1572872 | tf_op jit(solution)/shard_map/ppermute | solution.py:14
  372.6 22.7 %collective-permute-start.5 = (bf16[32,1,16,512]{3,0,2,1:T(8,128)(2,1)S(1)}, bf16[32,1,16,512]{3,0,2,1:T(8,128)(2,1)S(1)}, u32[]{:S(2)}, u32[]{:S(2)}) collective-permute-start(bf16[32,1,16,512]{3,0,2,1:T(8,128)(2,1)S(1)} %get-tuple-element.101), channel_id=1, source_target_pairs={{2,0},{4,2},{6,4},{8,6},{10,8},{12,10},{14,12},{3,1},{5,3},{7,5},{... | collective-permute-start | bytes 1572872 | tf_op jit(solution)/shard_map/ppermute | solution.py:15
  396.9 3.5 collective-permute-start.6
  399.1 4.4 collective-permute-start.7
where the time goes:
time: 617 us; the launch traced here: 613 us
  matrix products  291 us (47%)
  local copies, waits for them, and re-layouts  113 us (18%)
  blocking collectives  92.3 us (15%)
  other arithmetic  50.4 us (8%)
  waiting for transfers between devices  47.7 us (8%)
  starting transfers between devices  18.6 us (3%)
    dot_general x9, matrix products, aggregate(): jnp.einsum('koc,kcdhw->odhw', kernel, window, preferred_element_type=jnp....  263 us
    all_gather x3, blocking collectives, joined(): pieces = jax.tree.map(lambda part: lax.all_gather(part, axis), value)  92.3 us
    slice x2, local copies, waits for them, and re-layouts, regress(): tapped[9 * depth_tap + 3 * row_tap + col_tap, depth_tap:depth_tap + depth...  77.7 us
    ppermute x4, waiting for transfers between devices, padded(): before = lax.ppermute(last, axis, up)  42.3 us
    another operation x2, other arithmetic, aggregate(): jnp.stack([extended[:, :, :, col_tap:col_tap + out_cols] for col_tap in r...  37.5 us
    dot_general x1, matrix products, regress(): jnp.einsum('tc,cdhw->tdhw', reg_weight, extended, preferred_element_type=...  27.8 us
    another operation x1, local copies, waits for them, and re-layouts, aggregate(): jnp.stack([extended[:, :, :, col_tap:col_tap + out_cols] for col_tap in r...  18.4 us
    unnamed x11, local copies, waits for them, and re-layouts  13.6 us
  transfers between devices with their start and end apart: 8, of which 5 were waited for; matrix products, arithmetic and copies ran while one was open for 2% of the time, Pallas kernels for 0%

commit v1 on v0

v1 whole, which is shorter than its diff:
```python
import functools

import jax
import jax.numpy as jnp
from jax import lax
from jax.experimental import pallas as pl
from jax.experimental.pallas import tpu as pltpu
from jax.sharding import PartitionSpec as P

BF = jnp.bfloat16
F32 = jnp.float32


def shifted(x, axis, step):
    count = lax.axis_size(axis)
    pairs = [(i, i + step) for i in range(count) if 0 <= i + step < count]
    return lax.ppermute(x, axis, pairs)


def band_matrix(conv_weight, height):
    ch_out, ch = conv_weight.shape[1:]
    span = ch * height
    col = jnp.arange(span)
    spread = (col[None, :] // height == jnp.arange(ch)[:, None]).astype(BF)
    wide = jnp.einsum("toc,cg->tog", conv_weight, spread, preferred_element_type=F32).astype(BF)
    row = jnp.arange(height)
    masks = [(col[None, :] % height) == row[:, None] + b - 1 for b in range(3)]
    slots = []
    for a in range(3):
        parts = []
        for c in range(3):
            out = jnp.zeros((ch_out, height, span), BF)
            for b in range(3):
                out = jnp.where(masks[b][None], wide[9 * a + 3 * b + c][:, None, :], out)
            parts.append(out.reshape(ch_out * height, span))
        zero = jnp.zeros((ch_out, ch), BF)
        edges = []
        for c in range(3):
            edges += [conv_weight[9 * a + c], conv_weight[9 * a + 6 + c]]
        pad = edge_rows(ch) - 6 * ch
        edges += [jnp.zeros((ch_out, pad), BF)]
        edge = jnp.concatenate(edges, axis=1)
        ecol = jnp.arange(edge_rows(ch))
        side = (ecol // ch) % 2
        keep = row[:, None] == jnp.where(side == 0, 0, height - 1)[None, :]
        edge = jnp.where(keep[None], edge[:, None, :], jnp.zeros((), BF))
        parts.append(edge.reshape(ch_out * height, edge_rows(ch)))
        slots.append(parts)
    return jnp.concatenate([p for a in (0, 1, 2, 0, 1) for p in slots[a]], axis=1)


def edge_rows(ch):
    return -(-6 * ch // 256) * 256


def reg_matrix(reg_weight, height):
    ch = reg_weight.shape[1]
    span = ch * height
    col = jnp.arange(span)
    spread = (col[None, :] // height == jnp.arange(ch)[:, None]).astype(BF)
    wide = jnp.einsum("tc,cg->tg", reg_weight, spread, preferred_element_type=F32).astype(BF)
    row = jnp.arange(height + 8)
    place = jnp.where(row < height, row, jnp.where(row == height, -1, jnp.where(row == height + 1, height, -9)))
    out = []
    for a in range(3):
        for c in range(3):
            block = jnp.zeros((height + 8, span), BF)
            for b in range(3):
                mask = (col[None, :] % height) == place[:, None] + b - 1
                block = jnp.where(mask, wide[9 * a + 3 * b + c][None], block)
            out.append(block)
    return jnp.concatenate(out, axis=0)


def move(x, step):
    width = x.shape[1]
    rolled = pltpu.roll(x, step % width, 1)
    lane = lax.broadcasted_iota(jnp.int32, x.shape, 1)
    return jnp.where(lane == (0 if step == 1 else width - 1), jnp.zeros((), x.dtype), rolled)


def put_plane(x3, slot, x, e):
    span, es = x.shape[0], e.shape[0]
    depth = x3.shape[1]
    for k, step in enumerate((1, 0, -1)):
        if step:
            xs = move(x.astype(F32), step).astype(BF)
            es_ = move(e.astype(F32), step).astype(BF)
        else:
            xs, es_ = x, e
        x3[slot, k * span : (k + 1) * span, :] = xs
        x3[slot, 3 * span + k * es : 3 * span + (k + 1) * es, :] = es_
    tail = 3 * span + 3 * es
    if tail < depth:
        x3[slot, tail:depth, :] = jnp.zeros((depth - tail, x.shape[1]), BF)


def out_plane(phase, a_ref, x3, bias, r_ref, cost, at):
    slots, depth, width = x3.shape
    start = phase * depth if isinstance(phase, int) else pl.multiple_of(phase * depth, 128)
    a = a_ref[:, pl.ds(start, slots * depth)]
    x = x3[...].reshape(slots * depth, width)
    acc = jnp.dot(a, x, preferred_element_type=F32)
    hidden = jnp.maximum(acc + bias[...], 0.0).astype(BF)
    part = jnp.dot(r_ref[...], hidden, preferred_element_type=F32)
    rows = cost.shape[1]
    for tap in range(3):
        base = 3 * tap * rows
        total = (
            move(part[base : base + rows], 1)
            + part[base + rows : base + 2 * rows]
            + move(part[base + 2 * rows : base + 3 * rows], -1)
        )
        cost[at + 2 - tap] += total


def inner_kernel(v_ref, e_ref, a_ref, bias, r_ref, cost, x3):
    step = pl.program_id(0)

    @pl.when(step == 0)
    def _():
        cost[...] = jnp.zeros_like(cost)

    span = v_ref.shape[0] * v_ref.shape[2]
    put_plane(x3, lax.rem(step, 3), v_ref[:, 0].reshape(span, v_ref.shape[3]), e_ref[0])

    @pl.when(step >= 2)
    def _():
        first = lax.rem(step + 1, 3)
        out_plane(lax.rem(3 - first, 3), a_ref, x3, bias, r_ref, cost, step - 1)


def rim_kernel(planes, v_ref, e_ref, a_ref, bias, r_ref, cost_in, cost, x3):
    step = pl.program_id(0)

    @pl.when(step == 0)
    def _():
        cost[...] = cost_in[...]

    span = v_ref.shape[1] * v_ref.shape[2]
    put_plane(x3, lax.rem(step, 3), v_ref[0].reshape(span, v_ref.shape[3]), e_ref[0])

    @pl.when(lax.rem(step, 3) == 2)
    def _():
        out_plane(0, a_ref, x3, bias, r_ref, cost, jnp.where(step == 2, 0, planes - 1))


def combine(first, second):
    peak = jnp.maximum(first[0], second[0])
    left = jnp.exp(first[0] - peak)
    right = jnp.exp(second[0] - peak)
    return jnp.stack((peak, first[1] * left + second[1] * right, first[2] * left + second[2] * right))


def joined(value, axis):
    count = lax.axis_size(axis)
    if count & (count - 1):
        pieces = lax.all_gather(value, axis)
        running = pieces[0]
        for i in range(1, count):
            running = combine(running, pieces[i])
        return running
    step = 1
    while step < count:
        other = lax.ppermute(value, axis, [(i, i ^ step) for i in range(count)])
        value = combine(value, other)
        step *= 2
    return value


def body(volume, conv_weight, conv_bias, reg_weight):
    ch, planes, height, width = volume.shape
    span = ch * height
    rows = height + 8
    depth = 3 * span + edge_rows(ch)

    before = shifted(volume[:, planes - 1], "disp", 1)
    after = shifted(volume[:, 0], "disp", -1)
    above = shifted(jnp.swapaxes(volume[:, :, height - 1], 0, 1), "rows", 1)
    below = shifted(jnp.swapaxes(volume[:, :, 0], 0, 1), "rows", -1)
    edge = jnp.concatenate([above, below], axis=1)
    edge_before = shifted(edge[planes - 1], "disp", 1)
    edge_after = shifted(edge[0], "disp", -1)

    a = band_matrix(conv_weight, height)
    r = reg_matrix(reg_weight, height)
    bias = jnp.repeat(conv_bias, height)[:, None]

    def whole(x):
        return pl.BlockSpec(x.shape, lambda i: (0,) * x.ndim, pipeline_mode=pl.Buffered(1))

    cost_shape = jax.ShapeDtypeStruct((planes + 2, rows, width), F32)
    cost_spec = pl.BlockSpec(cost_shape.shape, lambda i: (0, 0, 0))
    scratch = [pltpu.VMEM((3, depth, width), BF)]
    params = pltpu.CompilerParams(vmem_limit_bytes=56 << 20, dimension_semantics=("arbitrary",))
    flops = 2 * span * 3 * depth * width

    cost = pl.pallas_call(
        inner_kernel,
        grid=(planes,),
        in_specs=[
            pl.BlockSpec((ch, 1, height, width), lambda i: (0, i, 0, 0)),
            pl.BlockSpec((1, 2 * ch, width), lambda i: (i, 0, 0)),
            whole(a),
            whole(bias),
            whole(r),
        ],
        out_specs=cost_spec,
        out_shape=cost_shape,
        scratch_shapes=scratch,
        compiler_params=params,
        cost_estimate=pl.CostEstimate(
            flops=(planes - 2) * flops, bytes_accessed=2 * volume.size, transcendentals=0
        ),
        name="inner",
    )(volume, edge, a, bias, r)

    rim_v = jnp.stack(
        [before, volume[:, 0], volume[:, 1], volume[:, planes - 2], volume[:, planes - 1], after]
    )
    rim_e = jnp.stack([edge_before, edge[0], edge[1], edge[planes - 2], edge[planes - 1], edge_after])
    cost = pl.pallas_call(
        functools.partial(rim_kernel, planes),
        grid=(6,),
        in_specs=[
            pl.BlockSpec((1, ch, height, width), lambda i: (i, 0, 0, 0)),
            pl.BlockSpec((1, 2 * ch, width), lambda i: (i, 0, 0)),
            whole(a),
            whole(bias),
            whole(r),
            whole(cost_shape),
        ],
        out_specs=cost_spec,
        out_shape=cost_shape,
        scratch_shapes=scratch,
        compiler_params=params,
        cost_estimate=pl.CostEstimate(flops=2 * flops, bytes_accessed=2 * rim_v.size, transcendentals=0),
        name="rim",
    )(rim_v, rim_e, a, bias, r, cost)

    from_before = shifted(cost[planes + 1], "disp", 1)
    from_after = shifted(cost[0], "disp", -1)
    cost = cost[1 : planes + 1]
    cost = cost.at[0].add(from_before).at[planes - 1].add(from_after)
    from_below = shifted(cost[:, height], "rows", -1)
    from_above = shifted(cost[:, height + 1], "rows", 1)
    cost = cost[:, :height]
    cost = cost.at[:, height - 1].add(from_below).at[:, 0].add(from_above)

    score = -cost
    peak = jnp.max(score, axis=0)
    expo = jnp.exp(score - peak[None])
    index = (lax.axis_index("disp") * planes + jnp.arange(planes, dtype=jnp.int32)).astype(F32)
    total = jnp.sum(expo, axis=0)
    moment = jnp.sum(index[:, None, None] * expo, axis=0)
    value = joined(jnp.stack((peak, total, moment)), "disp")
    return value[2] / value[1]


def solution(mesh):
    in_specs = (P(None, "disp", ("tiles", "rows"), None), P(), P(), P())
    out_specs = P(("tiles", "rows"), None)
    return jax.shard_map(body, mesh=mesh, in_specs=in_specs, out_specs=out_specs, check_vma=False)
```

time: 617 us -> 224 us (0.36)
  matrix products: 291 us -> 0.51 us
  Pallas kernels: 0 us -> 107 us
  blocking collectives: 92.3 us -> 0 us
  local copies, waits for them, and re-layouts: 113 us -> 51.6 us
  other arithmetic: 50.4 us -> 14.1 us
  waiting for transfers between devices: 47.7 us -> 15 us
  starting transfers between devices: 18.6 us -> 33.9 us
    dot_general x10 -> x2, matrix products: 291 us -> 0.51 us  [the longest x1 0.37 us: band_matrix(): jnp.einsum('toc,cg->tog', conv_weight, spread, preferred_element_type=F32)]
    pallas_call x0 -> x2, Pallas kernels: none -> 107 us  [the longest x1 90.5 us: body(): pl.pallas_call(inner_kernel, grid=(planes,), in_specs=[pl.BlockSpec((ch,...]
    all_gather x3 -> x0, blocking collectives: 92.3 us -> none  [joined(): pieces = jax.tree.map(lambda part: lax.all_gather(part, axis), value)]
    slice x11 -> x7, local copies, waits for them, and re-layouts: 80.5 us -> 10.8 us  [the longest x1 6.89 us: body(): below = shifted(jnp.swapaxes(volume[:, :, 0], 0, 1), 'rows', -1)]
    another operation x2 -> x4, other arithmetic: 37.5 us -> 0.84 us  [the longest x1 0.82 us: body(): jnp.stack([edge_before, edge[0], edge[1], edge[planes - 2], edge[planes -...]
    ppermute x8 -> x13, waiting for transfers between devices: 47.7 us -> 15 us  [the longest x3 9.28 us: joined(): other = lax.ppermute(value, axis, [(i, i ^ step) for i in range(count)])]
    unnamed x11 -> x40, local copies, waits for them, and re-layouts: 13.6 us -> 30.7 us
    another operation x1 -> x3, local copies, waits for them, and re-layouts: 18.4 us -> 1.97 us  [the longest x1 1.08 us: body(): jnp.stack([before, volume[:, 0], volume[:, 1], volume[:, planes - 2], vol...]
  transfers between devices with their start and end apart: 8 -> 13, of which waited for: 5 -> 5; matrix products, arithmetic and copies ran while one was open for 2% -> 24% of each run, Pallas kernels for 0% -> 41%
where the time goes in v1:
time: 224 us; the launch traced here: 222 us
  Pallas kernels  107 us (48%)
  local copies, waits for them, and re-layouts  51.6 us (23%)
  starting transfers between devices  33.9 us (15%)
  waiting for transfers between devices  15 us (7%)
  other arithmetic  14.1 us (6%)
    pallas_call x1, Pallas kernels, body(): pl.pallas_call(inner_kernel, grid=(planes,), in_specs=[pl.BlockSpec((ch,...  90.5 us
    unnamed x40, local copies, waits for them, and re-layouts  30.7 us
    ppermute x10, starting transfers between devices, shifted(): return lax.ppermute(x, axis, pairs)  26.9 us
    pallas_call x1, Pallas kernels, body(): pl.pallas_call(functools.partial(rim_kernel, planes), grid=(6,), in_specs...  16.2 us
    ppermute x3, waiting for transfers between devices, joined(): other = lax.ppermute(value, axis, [(i, i ^ step) for i in range(count)])  9.28 us
    ppermute x3, starting transfers between devices, joined(): other = lax.ppermute(value, axis, [(i, i ^ step) for i in range(count)])  7 us
    slice x1, local copies, waits for them, and re-layouts, body(): below = shifted(jnp.swapaxes(volume[:, :, 0], 0, 1), 'rows', -1)  6.89 us
    unnamed x8, other arithmetic  6.04 us
  transfers between devices with their start and end apart: 13, of which 5 were waited for; matrix products, arithmetic and copies ran while one was open for 24% of the time, Pallas kernels for 41%

profile of v1, /device:TPU:0, one launch (start us, length us, event | category | flops | bytes accessed | tf_op | source)
XLA Modules:
  0.0 222.3 jit_solution(16706662903666502117)
XLA Ops:
  0.0 6.9 %fusion.38 = (bf16[32,24,1,512]{3,2,1,0:T(2,128)(2,1)S(1)}, bf16[32,24,1,512]{3,2,1,0:T(2,128)(2,1)S(1)}) fusion(bf16[32,24,16,512]{3,2,1,0:T(8,128)(2,1)} %v_ref.1), kind=kLoop, calls=%fused_computation.257 | loop fusion | bytes 3145728 | tf_op jit(solution)/shard_map/slice | solution.py:180
  6.9 1.7 copy.43
  8.6 3.3 %collective-permute-start.2 = (bf16[24,32,512]{2,1,0:T(8,128)(2,1)}, bf16[24,32,512]{2,1,0:T(8,128)(2,1)}, u32[]{:S(2)}, u32[]{:S(2)}) collective-permute-start(bf16[24,32,512]{2,1,0:T(8,128)(2,1)} %bitcast.261), channel_id=1, source_target_pairs={{0,1},{2,3},{4,5},{6,7},{8,9},{10,11},{12,13},{14,15},{16,17},{18,... | collective-permute-start | bytes 2359304 | tf_op jit(solution)/shard_map/ppermute | solution.py:17
  12.0 1.7 copy.42
  15.0 2.2 %slice_bitcast_fusion = (bf16[32,16,512]{2,1,0:T(8,128)(2,1)}, bf16[32,16,512]{2,1,0:T(8,128)(2,1)}) fusion(bf16[32,24,16,512]{3,2,1,0:T(8,128)(2,1)} %v_ref.1), kind=kLoop, calls=%fused_computation.25 | loop fusion | bytes 2097152 | tf_op jit(solution)/shard_map/squeeze | solution.py:178
  17.2 5.0 %collective-permute-start = (bf16[32,16,512]{2,1,0:T(8,128)(2,1)}, bf16[32,16,512]{2,1,0:T(8,128)(2,1)}, u32[]{:S(2)}, u32[]{:S(2)}) collective-permute-start(bf16[32,16,512]{2,1,0:T(8,128)(2,1)} %get-tuple-element.87), channel_id=1, source_target_pairs={{0,2},{2,4},{4,6},{6,8},{8,10},{10,12},{12,14},{1,3},{3,5},{5,7},{... | collective-permute-start | bytes 1572872 | tf_op jit(solution)/shard_map/ppermute | solution.py:17
  26.4 1.5 select_select_fusion.1
  29.4 1.5 select_select_fusion
  39.2 2.0 constant_dynamic-update-slice_fusion.13
  41.2 1.9 constant_dynamic-update-slice_fusion.12
  43.1 1.9 constant_dynamic-update-slice_fusion.11
  67.7 1.8 constant_dynamic-update-slice_fusion.1
  70.8 4.6 %collective-permute-start.4 = (bf16[64,512]{1,0:T(8,128)(2,1)S(1)}, bf16[64,512]{1,0:T(8,128)(2,1)S(1)}, u32[]{:S(2)}, u32[]{:S(2)}) collective-permute-start(bf16[64,512]{1,0:T(8,128)(2,1)S(1)} %get-tuple-element.88), channel_id=1, source_target_pairs={{0,2},{2,4},{4,6},{6,8},{8,10},{10,12},{12,14},{1,3},{3,5},{5,7},{... | collective-permute-start | bytes 196616 | tf_op jit(solution)/shard_map/ppermute | solution.py:17
  76.6 90.5 %inner.1.cost_in = f32[26,24,512]{2,1,0:T(8,128)} custom-call(bf16[32,24,16,512]{3,2,1,0:T(8,128)(2,1)} %v_ref.1, bf16[24,64,512]{2,1,0:T(8,128)(2,1)} %copy-done.1, bf16[512,8960]{1,0:T(8,128)(2,1)} %constant_dynamic-update-slice_fusion.2.a_ref, f32[512,1]{1,0:T(8,128)} %broadcast_in_dim_reshape.4.bias, bf16[216,512]{1,0:T(8,128)(2,1)} %copy-done.4), custom_call_target="tpu_custom_call" | custom-call | flops 62008590336 | bytes 12582912 | tf_op jit(solution)/shard_map/inner/pallas_call | solution.py:198
  169.0 16.2 %rim.1 = f32[26,24,512]{2,1,0:T(8,128)} custom-call(bf16[6,32,16,512]{3,2,1,0:T(8,128)(2,1)} %copy-done.3, bf16[6,64,512]{2,1,0:T(8,128)(2,1)} %pad_maximum_fusion.e_ref, bf16[512,8960]{1,0:T(8,128)(2,1)} %constant_dynamic-update-slice_fusion.2.a_ref, f32[512,1]{1,0:T(8,128)} %broadcast_in_dim_reshape.4.bias, bf16[216,512]{1,0:T(8,128)(2,1)} %copy-done.4, ...), custom_call_target="tpu_custom_call" | custom-call | flops 5637144576 | bytes 3145728 | tf_op jit(solution)/shard_map/rim/pallas_call | solution.py:222
  186.0 4.5 %collective-permute-start.6 = (f32[24,512]{1,0:T(8,128)S(1)}, f32[24,512]{1,0:T(8,128)S(1)}, u32[]{:S(2)}, u32[]{:S(2)}) collective-permute-start(f32[24,512]{1,0:T(8,128)S(1)} %get-tuple-element.93), channel_id=1, source_target_pairs={{0,2},{2,4},{4,6},{6,8},{8,10},{10,12},{12,14},{1,3},{3,5},{5,7},{... | collective-permute-start | bytes 147464 | tf_op jit(solution)/shard_map/ppermute | solution.py:17
  194.0 4.8 %collective-permute-done.7 = f32[24,512]{1,0:T(8,128)S(1)} collective-permute-done((f32[24,512]{1,0:T(8,128)S(1)}, f32[24,512]{1,0:T(8,128)S(1)}, u32[]{:S(2)}, u32[]{:S(2)}) %collective-permute-start.7) | collective-permute-done | bytes 49184 | tf_op jit(solution)/shard_map/ppermute | solution.py:17
  200.8 3.0 %collective-permute-start.9 = (f32[24,512]{1,0:T(8,128)S(1)}, f32[24,512]{1,0:T(8,128)S(1)}, u32[]{:S(2)}, u32[]{:S(2)}) collective-permute-start(f32[24,512]{1,0:T(8,128)S(1)} %bitcast.290), channel_id=1, source_target_pairs={{0,1},{2,3},{4,5},{6,7},{8,9},{10,11},{12,13},{14,15},{16,17},{18,... | collective-permute-start | bytes 147464 | tf_op jit(solution)/shard_map/ppermute | solution.py:17
  205.2 2.7 %collective-permute-start.10 = (f32[3,16,512]{2,1,0:T(8,128)S(1)}, f32[3,16,512]{2,1,0:T(8,128)S(1)}, u32[]{:S(2)}, u32[]{:S(2)}) collective-permute-start(f32[3,16,512]{2,1,0:T(8,128)S(1)} %pad_maximum_fusion.1), channel_id=1, source_target_pairs={{0,2},{2,0},{4,6},{6,4},{8,10},{10,8},{12,14},{14,12},{1,3},{3,1},... | collective-permute-start | bytes 294920 | tf_op jit(solution)/shard_map/ppermute | solution.py:165
  207.9 3.3 %collective-permute-done.10 = f32[3,16,512]{2,1,0:T(8,128)S(1)} collective-permute-done((f32[3,16,512]{2,1,0:T(8,128)S(1)}, f32[3,16,512]{2,1,0:T(8,128)S(1)}, u32[]{:S(2)}, u32[]{:S(2)}) %collective-permute-start.10) | collective-permute-done | bytes 98336 | tf_op jit(solution)/shard_map/ppermute | solution.py:165
  211.3 1.6 collective-permute-start.11
  212.9 3.0 %collective-permute-done.11 = f32[3,16,512]{2,1,0:T(8,128)S(1)} collective-permute-done((f32[3,16,512]{2,1,0:T(8,128)S(1)}, f32[3,16,512]{2,1,0:T(8,128)S(1)}, u32[]{:S(2)}, u32[]{:S(2)}) %collective-permute-start.11) | collective-permute-done | bytes 98336 | tf_op jit(solution)/shard_map/ppermute | solution.py:165
  216.0 2.7 %collective-permute-start.12 = (f32[3,16,512]{2,1,0:T(8,128)S(1)}, f32[3,16,512]{2,1,0:T(8,128)S(1)}, u32[]{:S(2)}, u32[]{:S(2)}) collective-permute-start(f32[3,16,512]{2,1,0:T(8,128)S(1)} %pad_maximum_fusion.3), channel_id=1, source_target_pairs={{0,8},{2,10},{4,12},{6,14},{8,0},{10,2},{12,4},{14,6},{1,9},{3,11}... | collective-permute-start | bytes 294920 | tf_op jit(solution)/shard_map/ppermute | solution.py:165
  218.7 2.9 %collective-permute-done.12 = f32[3,16,512]{2,1,0:T(8,128)S(1)} collective-permute-done((f32[3,16,512]{2,1,0:T(8,128)S(1)}, f32[3,16,512]{2,1,0:T(8,128)S(1)}, u32[]{:S(2)}, u32[]{:S(2)}) %collective-permute-start.12) | collective-permute-done | bytes 98336 | tf_op jit(solution)/shard_map/ppermute | solution.py:165
  (103 shorter events, 50.3 us)
Async XLA Ops:
  0.0 24.7 %copy-start = (bf16[27,32]{1,0:T(8,128)(2,1)S(1)}, bf16[27,32]{1,0:T(8,128)(2,1)}, u32[]{:S(2)}) copy-start(bf16[27,32]{1,0:T(8,128)(2,1)} %param.15) | copy-start | bytes 5188
  0.0 23.6 %copy-start.2 = (bf16[27,32,32]{2,1,0:T(8,128)(2,1)S(1)}, bf16[27,32,32]{2,1,0:T(8,128)(2,1)}, u32[]{:S(2)}) copy-start(bf16[27,32,32]{2,1,0:T(8,128)(2,1)} %param.13) | copy-start | bytes 165892
  8.6 59.1 %collective-permute-start.2 = (bf16[24,32,512]{2,1,0:T(8,128)(2,1)}, bf16[24,32,512]{2,1,0:T(8,128)(2,1)}, u32[]{:S(2)}, u32[]{:S(2)}) collective-permute-start(bf16[24,32,512]{2,1,0:T(8,128)(2,1)} %bitcast.261), channel_id=1, source_target_pairs={{0,1},{2,3},{4,5},{6,7},{8,9},{10,11},{12,13},{14,15},{16,17},{18,... | collective-permute-start | bytes 2359304 | tf_op jit(solution)/shard_map/ppermute | solution.py:17
  13.7 55.8 %collective-permute-start.3 = (bf16[24,32,512]{2,1,0:T(8,128)(2,1)}, bf16[24,32,512]{2,1,0:T(8,128)(2,1)}, u32[]{:S(2)}, u32[]{:S(2)}) collective-permute-start(bf16[24,32,512]{2,1,0:T(8,128)(2,1)} %bitcast.260), channel_id=1, source_target_pairs={{1,0},{3,2},{5,4},{7,6},{9,8},{11,10},{13,12},{15,14},{17,16},{19,... | collective-permute-start | bytes 2359304 | tf_op jit(solution)/shard_map/ppermute | solution.py:17
  17.2 43.8 %collective-permute-start = (bf16[32,16,512]{2,1,0:T(8,128)(2,1)}, bf16[32,16,512]{2,1,0:T(8,128)(2,1)}, u32[]{:S(2)}, u32[]{:S(2)}) collective-permute-start(bf16[32,16,512]{2,1,0:T(8,128)(2,1)} %get-tuple-element.87), channel_id=1, source_target_pairs={{0,2},{2,4},{4,6},{6,8},{8,10},{10,12},{12,14},{1,3},{3,5},{5,7},{... | collective-permute-start | bytes 1572872 | tf_op jit(solution)/shard_map/ppermute | solution.py:17
  22.3 44.3 %collective-permute-start.1 = (bf16[32,16,512]{2,1,0:T(8,128)(2,1)}, bf16[32,16,512]{2,1,0:T(8,128)(2,1)}, u32[]{:S(2)}, u32[]{:S(2)}) collective-permute-start(bf16[32,16,512]{2,1,0:T(8,128)(2,1)} %get-tuple-element.86), channel_id=1, source_target_pairs={{2,0},{4,2},{6,4},{8,6},{10,8},{12,10},{14,12},{3,1},{5,3},{7,5},{... | collective-permute-start | bytes 1572872 | tf_op jit(solution)/shard_map/ppermute | solution.py:17
  61.1 15.6 %copy-start.4 = (bf16[216,512]{1,0:T(8,128)(2,1)}, bf16[216,512]{1,0:T(8,128)(2,1)S(1)}, u32[]{:S(2)}) copy-start(bf16[216,512]{1,0:T(8,128)(2,1)S(1)} %constant_dynamic-update-slice_fusion.22.r_ref) | copy-start | bytes 663556
  67.7 99.4 %copy-start.3 = (bf16[6,32,16,512]{3,2,1,0:T(8,128)(2,1)}, bf16[6,32,16,512]{3,2,1,0:T(8,128)(2,1)S(1)}, u32[]{:S(2)}) copy-start(bf16[6,32,16,512]{3,2,1,0:T(8,128)(2,1)S(1)} %bitcast_dynamic-update-slice_fusion.4.v_ref) | copy-start | bytes 9437188
  70.7 5.9 %copy-start.1 = (bf16[24,64,512]{2,1,0:T(8,128)(2,1)}, bf16[24,64,512]{2,1,0:T(8,128)(2,1)S(1)}, u32[]{:S(2)}) copy-start(bf16[24,64,512]{2,1,0:T(8,128)(2,1)S(1)} %constant_dynamic-update-slice_fusion.e_ref) | copy-start | bytes 4718596
  70.8 97.4 %collective-permute-start.4 = (bf16[64,512]{1,0:T(8,128)(2,1)S(1)}, bf16[64,512]{1,0:T(8,128)(2,1)S(1)}, u32[]{:S(2)}, u32[]{:S(2)}) collective-permute-start(bf16[64,512]{1,0:T(8,128)(2,1)S(1)} %get-tuple-element.88), channel_id=1, source_target_pairs={{0,2},{2,4},{4,6},{6,8},{8,10},{10,12},{12,14},{1,3},{3,5},{5,7},{... | collective-permute-start | bytes 196616 | tf_op jit(solution)/shard_map/ppermute | solution.py:17
  75.3 92.8 %collective-permute-start.5 = (bf16[64,512]{1,0:T(8,128)(2,1)S(1)}, bf16[64,512]{1,0:T(8,128)(2,1)S(1)}, u32[]{:S(2)}, u32[]{:S(2)}) collective-permute-start(bf16[64,512]{1,0:T(8,128)(2,1)S(1)} %get-tuple-element.89), channel_id=1, source_target_pairs={{2,0},{4,2},{6,4},{8,6},{10,8},{12,10},{14,12},{3,1},{5,3},{7,5},{... | collective-permute-start | bytes 196616 | tf_op jit(solution)/shard_map/ppermute | solution.py:17
  186.0 7.2 %collective-permute-start.6 = (f32[24,512]{1,0:T(8,128)S(1)}, f32[24,512]{1,0:T(8,128)S(1)}, u32[]{:S(2)}, u32[]{:S(2)}) collective-permute-start(f32[24,512]{1,0:T(8,128)S(1)} %get-tuple-element.93), channel_id=1, source_target_pairs={{0,2},{2,4},{4,6},{6,8},{8,10},{10,12},{12,14},{1,3},{3,5},{5,7},{... | collective-permute-start | bytes 147464 | tf_op jit(solution)/shard_map/ppermute | solution.py:17
  191.9 7.0 %collective-permute-start.7 = (f32[24,512]{1,0:T(8,128)S(1)}, f32[24,512]{1,0:T(8,128)S(1)}, u32[]{:S(2)}, u32[]{:S(2)}) collective-permute-start(f32[24,512]{1,0:T(8,128)S(1)} %get-tuple-element.92), channel_id=1, source_target_pairs={{2,0},{4,2},{6,4},{8,6},{10,8},{12,10},{14,12},{3,1},{5,3},{7,5},{... | collective-permute-start | bytes 147464 | tf_op jit(solution)/shard_map/ppermute | solution.py:17
  199.0 4.9 %collective-permute-start.8 = (f32[24,512]{1,0:T(8,128)S(1)}, f32[24,512]{1,0:T(8,128)S(1)}, u32[]{:S(2)}, u32[]{:S(2)}) collective-permute-start(f32[24,512]{1,0:T(8,128)S(1)} %bitcast.289), channel_id=1, source_target_pairs={{1,0},{3,2},{5,4},{7,6},{9,8},{11,10},{13,12},{15,14},{17,16},{19,... | collective-permute-start | bytes 147464 | tf_op jit(solution)/shard_map/ppermute | solution.py:17
  200.8 3.9 %collective-permute-start.9 = (f32[24,512]{1,0:T(8,128)S(1)}, f32[24,512]{1,0:T(8,128)S(1)}, u32[]{:S(2)}, u32[]{:S(2)}) collective-permute-start(f32[24,512]{1,0:T(8,128)S(1)} %bitcast.290), channel_id=1, source_target_pairs={{0,1},{2,3},{4,5},{6,7},{8,9},{10,11},{12,13},{14,15},{16,17},{18,... | collective-permute-start | bytes 147464 | tf_op jit(solution)/shard_map/ppermute | solution.py:17
  205.2 6.0 %collective-permute-start.10 = (f32[3,16,512]{2,1,0:T(8,128)S(1)}, f32[3,16,512]{2,1,0:T(8,128)S(1)}, u32[]{:S(2)}, u32[]{:S(2)}) collective-permute-start(f32[3,16,512]{2,1,0:T(8,128)S(1)} %pad_maximum_fusion.1), channel_id=1, source_target_pairs={{0,2},{2,0},{4,6},{6,4},{8,10},{10,8},{12,14},{14,12},{1,3},{3,1},... | collective-permute-start | bytes 294920 | tf_op jit(solution)/shard_map/ppermute | solution.py:165
  211.3 4.7 %collective-permute-start.11 = (f32[3,16,512]{2,1,0:T(8,128)S(1)}, f32[3,16,512]{2,1,0:T(8,128)S(1)}, u32[]{:S(2)}, u32[]{:S(2)}) collective-permute-start(f32[3,16,512]{2,1,0:T(8,128)S(1)} %pad_maximum_fusion.2), channel_id=1, source_target_pairs={{0,4},{2,6},{4,0},{6,2},{8,12},{10,14},{12,8},{14,10},{1,5},{3,7},... | collective-permute-start | bytes 294920 | tf_op jit(solution)/shard_map/ppermute | solution.py:165
  216.0 5.6 %collective-permute-start.12 = (f32[3,16,512]{2,1,0:T(8,128)S(1)}, f32[3,16,512]{2,1,0:T(8,128)S(1)}, u32[]{:S(2)}, u32[]{:S(2)}) collective-permute-start(f32[3,16,512]{2,1,0:T(8,128)S(1)} %pad_maximum_fusion.3), channel_id=1, source_target_pairs={{0,8},{2,10},{4,12},{6,14},{8,0},{10,2},{12,4},{14,6},{1,9},{3,11}... | collective-permute-start | bytes 294920 | tf_op jit(solution)/shard_map/ppermute | solution.py:165

commit v2 on v1

v2 whole, which is shorter than its diff:
```python
import functools

import jax
import jax.numpy as jnp
from jax import lax
from jax.experimental import pallas as pl
from jax.experimental.pallas import tpu as pltpu
from jax.sharding import PartitionSpec as P

BF = jnp.bfloat16
F32 = jnp.float32


def shifted(x, axis, step):
    count = lax.axis_size(axis)
    pairs = [(i, i + step) for i in range(count) if 0 <= i + step < count]
    return lax.ppermute(x, axis, pairs)


def edge_rows(ch):
    return -(-6 * ch // 256) * 256


def spread(rows, half):
    ch = rows.shape[-1]
    col = jnp.arange(ch * half)
    onehot = (col[None, :] // half == jnp.arange(ch)[:, None]).astype(BF)
    return jnp.einsum("...c,cg->...g", rows, onehot, preferred_element_type=F32)


def prep_kernel(v_ref, wide, wedge, wreg, last, first, local, a_ref, r_ref, pick):
    ch, count, height, width = v_ref.shape
    half = height // 2
    span = ch * half
    depth = 3 * span + edge_rows(ch)

    @pl.when(pl.program_id(0) == 0)
    def _():
        row = lax.broadcasted_iota(jnp.int32, pick.shape, 0)
        col = lax.broadcasted_iota(jnp.int32, pick.shape, 1)
        kind = row // ch
        at = jnp.where(kind == 0, height - 1, jnp.where(kind == 1, 0, jnp.where(kind == 2, half, half - 1)))
        pick[...] = (col == (row % ch) * height + at).astype(F32).astype(BF)

        shape = (ch, half, span)
        diff = lax.broadcasted_iota(jnp.int32, shape, 2) % half - lax.broadcasted_iota(jnp.int32, shape, 1)
        eshape = (ch, half, edge_rows(ch))
        side = (lax.broadcasted_iota(jnp.int32, eshape, 2) // ch) % 2
        keep = lax.broadcasted_iota(jnp.int32, eshape, 1) == side * (half - 1)
        for a in range(3):
            for c in range(3):
                out = jnp.zeros(shape, F32)
                for b in range(3):
                    line = jnp.broadcast_to(wide[9 * a + 3 * b + c][:, None, :], shape)
                    out = jnp.where(diff == b - 1, line, out)
                block = out.reshape(span, span).astype(BF)
                for slot in (a, a + 3):
                    if slot < 5:
                        a_ref[:, slot * depth + c * span : slot * depth + (c + 1) * span] = block
            line = jnp.broadcast_to(wedge[a][:, None, :], eshape)
            block = jnp.where(keep, line, 0.0).reshape(span, edge_rows(ch)).astype(BF)
            for slot in (a, a + 3):
                if slot < 5:
                    a_ref[:, slot * depth + 3 * span : (slot + 1) * depth] = block

        rshape = (height + 8, 2 * span)
        row = lax.broadcasted_iota(jnp.int32, rshape, 0)
        col = lax.broadcasted_iota(jnp.int32, rshape, 1)
        place = jnp.where(
            row < height, row, jnp.where(row == height, -1, jnp.where(row == height + 1, height, -9))
        )
        diff = (col // span) * half + col % half - place
        blocks = []
        for a in range(3):
            for c in range(3):
                out = jnp.zeros(rshape, F32)
                for b in range(3):
                    t = 9 * a + 3 * b + c
                    out = jnp.where(diff == b - 1, jnp.broadcast_to(wreg[t : t + 1, :], rshape), out)
                blocks.append(out)
        r_ref[...] = jnp.concatenate(blocks, axis=0).astype(BF)

    for p in range(count):
        x = v_ref[:, p].reshape(ch * height, width)
        rows = jnp.dot(pick[...], x, preferred_element_type=F32).astype(BF)
        last[p] = rows[:ch]
        first[p] = rows[ch : 2 * ch]
        local[p] = rows[2 * ch :]


def move(x, step):
    width = x.shape[1]
    rolled = pltpu.roll(x, step % width, 1)
    lane = lax.broadcasted_iota(jnp.int32, x.shape, 1)
    return jnp.where(lane == (0 if step == 1 else width - 1), jnp.zeros((), x.dtype), rolled)


def moved(x, step):
    return move(x.astype(F32), step).astype(BF) if step else x


def put_half(x3, slot, x, top, bottom):
    span, ch = x.shape[0], top.shape[0]
    depth = x3.shape[1]
    for k, step in enumerate((1, 0, -1)):
        x3[slot, k * span : (k + 1) * span, :] = moved(x, step)
        base = 3 * span + 2 * k * ch
        x3[slot, base : base + ch, :] = moved(top, step)
        x3[slot, base + ch : base + 2 * ch, :] = moved(bottom, step)
    tail = 3 * span + 6 * ch
    if tail < depth:
        x3[slot, tail:depth, :] = jnp.zeros((depth - tail, x.shape[1]), BF)


def out_plane(phase, a_ref, halves, bias, r_ref, cost, at):
    slots, depth, width = halves[0].shape
    start = phase * depth if isinstance(phase, int) else pl.multiple_of(phase * depth, 128)
    hidden = []
    for x3 in halves:
        a = a_ref[:, pl.ds(start, slots * depth)]
        acc = jnp.dot(a, x3[...].reshape(slots * depth, width), preferred_element_type=F32)
        hidden.append(jnp.maximum(acc + bias[...], 0.0).astype(BF))
    part = jnp.dot(r_ref[...], jnp.concatenate(hidden, axis=0), preferred_element_type=F32)
    rows = cost.shape[1]
    for tap in range(3):
        base = 3 * tap * rows
        total = (
            move(part[base : base + rows], 1)
            + part[base + rows : base + 2 * rows]
            + move(part[base + 2 * rows : base + 3 * rows], -1)
        )
        cost[at + 2 - tap] += total


def flat(x):
    return x.reshape(x.shape[0] * x.shape[1], x.shape[2])


def inner_kernel(lo, hi, above, local, below, a_ref, bias, r_ref, cost, x_lo, x_hi):
    step = pl.program_id(0)
    ch = above.shape[1]

    @pl.when(step == 0)
    def _():
        cost[...] = jnp.zeros_like(cost)

    slot = lax.rem(step, 3)
    put_half(x_lo, slot, flat(lo[:, 0]), above[0], local[0, :ch])
    put_half(x_hi, slot, flat(hi[:, 0]), local[0, ch:], below[0])

    @pl.when(step >= 2)
    def _():
        first = lax.rem(step + 1, 3)
        out_plane(lax.rem(3 - first, 3), a_ref, (x_lo, x_hi), bias, r_ref, cost, step - 1)


def rim_kernel(planes, lo, hi, b_lo, b_hi, a_lo, a_hi, e_ref, a_ref, bias, r_ref, cost_in, cost, x_lo, x_hi):
    step = pl.program_id(0)
    ch = lo.shape[0]

    @pl.when(step == 0)
    def _():
        cost[...] = cost_in[...]

    slot = lax.rem(step, 3)

    def put(low, high):
        put_half(x_lo, slot, flat(low), e_ref[0, :ch], e_ref[0, ch : 2 * ch])
        put_half(x_hi, slot, flat(high), e_ref[0, 2 * ch : 3 * ch], e_ref[0, 3 * ch :])

    @pl.when(step == 0)
    def _():
        put(b_lo[...], b_hi[...])

    @pl.when(step == 5)
    def _():
        put(a_lo[...], a_hi[...])

    @pl.when((step != 0) & (step != 5))
    def _():
        put(lo[:, 0], hi[:, 0])

    @pl.when(slot == 2)
    def _():
        out_plane(0, a_ref, (x_lo, x_hi), bias, r_ref, cost, jnp.where(step == 2, 0, planes - 1))


def combine(first, second):
    peak = jnp.maximum(first[0], second[0])
    left = jnp.exp(first[0] - peak)
    right = jnp.exp(second[0] - peak)
    return jnp.stack((peak, first[1] * left + second[1] * right, first[2] * left + second[2] * right))


def joined(value, axis):
    count = lax.axis_size(axis)
    if count & (count - 1):
        pieces = lax.all_gather(value, axis)
        running = pieces[0]
        for i in range(1, count):
            running = combine(running, pieces[i])
        return running
    step = 1
    while step < count:
        other = lax.ppermute(value, axis, [(i, i ^ step) for i in range(count)])
        value = combine(value, other)
        step *= 2
    return value


def body(volume, conv_weight, conv_bias, reg_weight):
    ch, planes, height, width = volume.shape
    half = height // 2
    span = ch * half
    rows = height + 8
    depth = 3 * span + edge_rows(ch)

    def whole(x):
        return pl.BlockSpec(x.shape, lambda i: (0,) * len(x.shape), pipeline_mode=pl.Buffered(1))

    def shape(*dims, dtype=BF):
        return jax.ShapeDtypeStruct(dims, dtype)

    before = shifted(volume[:, planes - 1], "disp", 1)
    after = shifted(volume[:, 0], "disp", -1)

    wide = spread(conv_weight, half)
    taps = jnp.transpose(conv_weight.reshape(3, 3, 3, ch, ch)[:, ::2], (0, 3, 2, 1, 4)).reshape(3, ch, 6 * ch)
    wedge = jnp.pad(taps, ((0, 0), (0, 0), (0, edge_rows(ch) - 6 * ch))).astype(F32)
    wreg = jnp.tile(spread(reg_weight, half), (1, 2))
    bias = jnp.repeat(conv_bias, half)[:, None]

    group = next(n for n in (4, 3, 2, 1) if planes % n == 0)
    last, first, local, a, r = pl.pallas_call(
        prep_kernel,
        grid=(planes // group,),
        in_specs=[
            pl.BlockSpec((ch, group, height, width), lambda i: (0, i, 0, 0)),
            whole(wide),
            whole(wedge),
            whole(wreg),
        ],
        out_specs=[
            pl.BlockSpec((group, ch, width), lambda i: (i, 0, 0)),
            pl.BlockSpec((group, ch, width), lambda i: (i, 0, 0)),
            pl.BlockSpec((group, 2 * ch, width), lambda i: (i, 0, 0)),
            pl.BlockSpec((span, 5 * depth), lambda i: (0, 0)),
            pl.BlockSpec((9 * rows, 2 * span), lambda i: (0, 0)),
        ],
        out_shape=[
            shape(planes, ch, width),
            shape(planes, ch, width),
            shape(planes, 2 * ch, width),
            shape(span, 5 * depth),
            shape(9 * rows, 2 * span),
        ],
        scratch_shapes=[pltpu.VMEM((4 * ch, ch * height), BF)],
        compiler_params=pltpu.CompilerParams(vmem_limit_bytes=48 << 20),
        cost_estimate=pl.CostEstimate(
            flops=8 * ch * ch * height * width * planes, bytes_accessed=2 * volume.size, transcendentals=0
        ),
        name="prep",
    )(volume, wide, wedge, wreg)

    above = shifted(last, "rows", 1)
    below = shifted(first, "rows", -1)

    def edges(p):
        return jnp.concatenate([above[p], local[p], below[p]], axis=0)

    head, foot = edges(0), edges(planes - 1)
    edge_before = shifted(foot, "disp", 1)
    edge_after = shifted(head, "disp", -1)

    cost_shape = shape(planes + 2, rows, width, dtype=F32)
    cost_spec = pl.BlockSpec(cost_shape.shape, lambda i: (0, 0, 0))
    scratch = [pltpu.VMEM((3, depth, width), BF)] * 2
    params = pltpu.CompilerParams(vmem_limit_bytes=48 << 20)
    flops = 4 * span * 3 * depth * width

    cost = pl.pallas_call(
        inner_kernel,
        grid=(planes,),
        in_specs=[
            pl.BlockSpec((ch, 1, half, width), lambda i: (0, i, 0, 0)),
            pl.BlockSpec((ch, 1, half, width), lambda i: (0, i, 1, 0)),
            pl.BlockSpec((1, ch, width), lambda i: (i, 0, 0)),
            pl.BlockSpec((1, 2 * ch, width), lambda i: (i, 0, 0)),
            pl.BlockSpec((1, ch, width), lambda i: (i, 0, 0)),
            whole(a),
            whole(bias),
            whole(r),
        ],
        out_specs=cost_spec,
        out_shape=cost_shape,
        scratch_shapes=scratch,
        compiler_params=params,
        cost_estimate=pl.CostEstimate(
            flops=(planes - 2) * flops, bytes_accessed=2 * volume.size, transcendentals=0
        ),
        name="inner",
    )(volume, volume, above, local, below, a, bias, r)

    def rim_plane(i):
        return jnp.where(i < 3, jnp.maximum(i - 1, 0), jnp.minimum(planes + i - 5, planes - 1))

    rim_e = jnp.stack([edge_before, head, edges(1), edges(planes - 2), foot, edge_after])
    cost = pl.pallas_call(
        functools.partial(rim_kernel, planes),
        grid=(6,),
        in_specs=[
            pl.BlockSpec((ch, 1, half, width), lambda i: (0, rim_plane(i), 0, 0)),
            pl.BlockSpec((ch, 1, half, width), lambda i: (0, rim_plane(i), 1, 0)),
            pl.BlockSpec((ch, half, width), lambda i: (0, 0, 0), pipeline_mode=pl.Buffered(1)),
            pl.BlockSpec((ch, half, width), lambda i: (0, 1, 0), pipeline_mode=pl.Buffered(1)),
            pl.BlockSpec((ch, half, width), lambda i: (0, 0, 0), pipeline_mode=pl.Buffered(1)),
            pl.BlockSpec((ch, half, width), lambda i: (0, 1, 0), pipeline_mode=pl.Buffered(1)),
            pl.BlockSpec((1, 4 * ch, width), lambda i: (i, 0, 0)),
            whole(a),
            whole(bias),
            whole(r),
            whole(cost_shape),
        ],
        out_specs=cost_spec,
        out_shape=cost_shape,
        scratch_shapes=scratch,
        compiler_params=params,
        cost_estimate=pl.CostEstimate(flops=2 * flops, bytes_accessed=2 * volume.size // 4, transcendentals=0),
        name="rim",
    )(volume, volume, before, before, after, after, rim_e, a, bias, r, cost)

    from_before = shifted(cost[planes + 1], "disp", 1)
    from_after = shifted(cost[0], "disp", -1)
    cost = cost[1 : planes + 1]
    cost = cost.at[0].add(from_before).at[planes - 1].add(from_after)
    from_below = shifted(cost[:, height], "rows", -1)
    from_above = shifted(cost[:, height + 1], "rows", 1)
    cost = cost[:, :height]
    cost = cost.at[:, height - 1].add(from_below).at[:, 0].add(from_above)

    score = -cost
    peak = jnp.max(score, axis=0)
    expo = jnp.exp(score - peak[None])
    index = (lax.axis_index("disp") * planes + jnp.arange(planes, dtype=jnp.int32)).astype(F32)
    total = jnp.sum(expo, axis=0)
    moment = jnp.sum(index[:, None, None] * expo, axis=0)
    value = joined(jnp.stack((peak, total, moment)), "disp")
    return value[2] / value[1]


def solution(mesh):
    in_specs = (P(None, "disp", ("tiles", "rows"), None), P(), P(), P())
    out_specs = P(("tiles", "rows"), None)
    return jax.shard_map(body, mesh=mesh, in_specs=in_specs, out_specs=out_specs, check_vma=False)
```

time: 224 us -> 139 us (0.62)
  local copies, waits for them, and re-layouts: 51.6 us -> 5 us
  Pallas kernels: 107 us -> 80.8 us
  other arithmetic: 14.1 us -> 1.34 us
    unnamed x40 -> x13, local copies, waits for them, and re-layouts: 30.7 us -> 0.64 us
    pallas_call x1, Pallas kernels: 90.5 us -> 60.8 us  [body(): pl.pallas_call(inner_kernel, grid=(planes,), in_specs=[pl.BlockSpec((ch,...]
    pallas_call x0 -> x1, Pallas kernels: none -> 9.62 us  [body(): pl.pallas_call(prep_kernel, grid=(planes // group,), in_specs=[pl.BlockSp...]
    slice x4 -> x1, local copies, waits for them, and re-layouts: 9.27 us -> 0.01 us  [body(): conv_weight.reshape(3, 3, 3, ch, ch)[:, ::2]]
    unnamed x8 -> x4, other arithmetic: 6.04 us -> 0.05 us
    pallas_call x1, Pallas kernels: 16.2 us -> 10.4 us  [body(): pl.pallas_call(functools.partial(rim_kernel, planes), grid=(6,), in_specs...]
    select_n x7 -> x1, other arithmetic: 3.74 us -> 0.01 us  [spread(): onehot = (col[None, :] // half == jnp.arange(ch)[:, None]).astype(BF)]
    concatenate x5 -> x0, local copies, waits for them, and re-layouts: 3.65 us -> none  [the longest x3 1.72 us: band_matrix(): edge = jnp.concatenate(edges, axis=1)]
  transfers between devices with their start and end apart: 13 -> 13, of which waited for: 5 -> 6; matrix products, arithmetic and copies ran while one was open for 24% -> 3% of each run, Pallas kernels for 41% -> 44%
where the time goes in v2:
time: 139 us
  Pallas kernels  80.8 us (58%)
  starting transfers between devices  33.6 us (24%)
  waiting for transfers between devices  16.2 us (12%)
  local copies, waits for them, and re-layouts  5 us (4%)
    pallas_call x1, Pallas kernels, body(): pl.pallas_call(inner_kernel, grid=(planes,), in_specs=[pl.BlockSpec((ch,...  60.8 us
    ppermute x10, starting transfers between devices, shifted(): return lax.ppermute(x, axis, pairs)  26.6 us
    pallas_call x1, Pallas kernels, body(): pl.pallas_call(functools.partial(rim_kernel, planes), grid=(6,), in_specs...  10.4 us
    pallas_call x1, Pallas kernels, body(): pl.pallas_call(prep_kernel, grid=(planes // group,), in_specs=[pl.BlockSp...  9.62 us
    ppermute x3, waiting for transfers between devices, joined(): other = lax.ppermute(value, axis, [(i, i ^ step) for i in range(count)])  9.31 us
    ppermute x3, starting transfers between devices, joined(): other = lax.ppermute(value, axis, [(i, i ^ step) for i in range(count)])  6.97 us
    ppermute x10, waiting for transfers between devices, shifted(): return lax.ppermute(x, axis, pairs)  6.87 us
  transfers between devices with their start and end apart: 13, of which 6 were waited for; matrix products, arithmetic and copies ran while one was open for 3% of the time, Pallas kernels for 44%

profile of v2, /device:TPU:0, one launch (start us, length us, event | category | flops | bytes accessed | tf_op | source)
XLA Modules:
  0.0 138.7 jit_solution(16185633368718788766)
XLA Ops:
  0.0 1.3 convolution_bitcast_fusion.wide
  1.8 9.6 %prep.1 = (bf16[24,32,512]{2,1,0:T(8,128)(2,1)}, bf16[24,32,512]{2,1,0:T(8,128)(2,1)}, bf16[24,64,512]{2,1,0:T(8,128)(2,1)S(1)}, bf16[256,5120]{1,0:T(8,128)(2,1)}, bf16[216,512]{1,0:T(8,128)(2,1)S(1)}) custom-call(bf16[32,24,16,512]{3,2,1,0:T(8,128)(2,1)} %hi.3, f32[27,32,256]{2,1,0:T(8,128)S(1)} %convolution_bitcast_fusion.wide, ...), custom_call_target="tpu_custom_call" | custom-call | flops 1610612736 | bytes 12582912 | tf_op jit(solution)/shard_map/prep/pallas_call | solution.py:234
  11.4 3.4 %collective-permute-start.2 = (bf16[24,32,512]{2,1,0:T(8,128)(2,1)}, bf16[24,32,512]{2,1,0:T(8,128)(2,1)}, u32[]{:S(2)}, u32[]{:S(2)}) collective-permute-start(bf16[24,32,512]{2,1,0:T(8,128)(2,1)} %get-tuple-element.58), channel_id=1, source_target_pairs={{0,1},{2,3},{4,5},{6,7},{8,9},{10,11},{12,13},{14,15},{16,17},{18,... | collective-permute-start | bytes 2359304 | tf_op jit(solution)/shard_map/ppermute | solution.py:17
  14.9 1.3 collective-permute-start.3
  16.1 2.1 %slice_bitcast_fusion = (bf16[32,16,512]{2,1,0:T(8,128)(2,1)S(1)}, bf16[32,16,512]{2,1,0:T(8,128)(2,1)}) fusion(bf16[32,24,16,512]{3,2,1,0:T(8,128)(2,1)} %hi.3), kind=kLoop, calls=%fused_computation.6 | loop fusion | bytes 2097152 | tf_op jit(solution)/shard_map/squeeze | solution.py:225
  18.2 4.3 %collective-permute-start = (bf16[32,16,512]{2,1,0:T(8,128)(2,1)}, bf16[32,16,512]{2,1,0:T(8,128)(2,1)S(1)}, u32[]{:S(2)}, u32[]{:S(2)}) collective-permute-start(bf16[32,16,512]{2,1,0:T(8,128)(2,1)} %get-tuple-element.68), channel_id=1, source_target_pairs={{0,2},{2,4},{4,6},{6,8},{8,10},{10,12},{12,14},{1,3},{3,5},{5,7},{... | collective-permute-start | bytes 1572872 | tf_op jit(solution)/shard_map/ppermute | solution.py:17
  22.5 1.3 collective-permute-start.1
  24.0 0.8 slice_bitcast_fusion.12
  25.7 4.6 %collective-permute-start.4 = (bf16[128,512]{1,0:T(8,128)(2,1)S(1)}, bf16[128,512]{1,0:T(8,128)(2,1)S(1)}, u32[]{:S(2)}, u32[]{:S(2)}) collective-permute-start(bf16[128,512]{1,0:T(8,128)(2,1)S(1)} %pad_maximum_fusion), channel_id=1, source_target_pairs={{0,2},{2,4},{4,6},{6,8},{8,10},{10,12},{12,14},{1,3},{3,5},{5,7},{... | collective-permute-start | bytes 393224 | tf_op jit(solution)/shard_map/ppermute | solution.py:17
  30.3 1.3 collective-permute-start.5
  31.6 60.8 %inner.1.cost_in = f32[26,24,512]{2,1,0:T(8,128)S(1)} custom-call(bf16[32,24,16,512]{3,2,1,0:T(8,128)(2,1)} %hi.3, bf16[32,24,16,512]{3,2,1,0:T(8,128)(2,1)} %hi.3, bf16[24,32,512]{2,1,0:T(8,128)(2,1)} %collective-permute-done.2.above, bf16[24,64,512]{2,1,0:T(8,128)(2,1)S(1)} %get-tuple-element.59.local, bf16[24,32,512]{2,1,0:T(8,128)(2,1)} %collective-permute-done.3.below, ...), custom_call_target="tpu_custom_call" | custom-call | flops 35433480192 | bytes 12582912 | tf_op jit(solution)/shard_map/inner/pallas_call | solution.py:281
  92.5 10.4 %rim.1 = f32[26,24,512]{2,1,0:T(8,128)S(1)} custom-call(bf16[32,24,16,512]{3,2,1,0:T(8,128)(2,1)} %hi.3, bf16[32,24,16,512]{3,2,1,0:T(8,128)(2,1)} %hi.3, bf16[32,16,512]{2,1,0:T(8,128)(2,1)S(1)} %collective-permute-done.b_lo.b_hi, bf16[32,16,512]{2,1,0:T(8,128)(2,1)S(1)} %collective-permute-done.b_lo.b_hi, ...), custom_call_target="tpu_custom_call" | custom-call | flops 3221225472 | bytes 3145728 | tf_op jit(solution)/shard_map/rim/pallas_call | solution.py:308
  102.9 4.9 %collective-permute-start.6 = (f32[24,512]{1,0:T(8,128)S(1)}, f32[24,512]{1,0:T(8,128)S(1)}, u32[]{:S(2)}, u32[]{:S(2)}) collective-permute-start(f32[24,512]{1,0:T(8,128)S(1)} %get-tuple-element.74), channel_id=1, source_target_pairs={{0,2},{2,4},{4,6},{6,8},{8,10},{10,12},{12,14},{1,3},{3,5},{5,7},{... | collective-permute-start | bytes 147464 | tf_op jit(solution)/shard_map/ppermute | solution.py:17
  107.9 1.3 collective-permute-start.7
  109.7 5.6 %collective-permute-done.7 = f32[24,512]{1,0:T(8,128)S(1)} collective-permute-done((f32[24,512]{1,0:T(8,128)S(1)}, f32[24,512]{1,0:T(8,128)S(1)}, u32[]{:S(2)}, u32[]{:S(2)}) %collective-permute-start.7) | collective-permute-done | bytes 49184 | tf_op jit(solution)/shard_map/ppermute | solution.py:17
  115.4 1.3 collective-permute-start.8
  117.2 3.0 %collective-permute-start.9 = (f32[24,512]{1,0:T(8,128)S(1)}, f32[24,512]{1,0:T(8,128)S(1)}, u32[]{:S(2)}, u32[]{:S(2)}) collective-permute-start(f32[24,512]{1,0:T(8,128)S(1)} %bitcast.183), channel_id=1, source_target_pairs={{0,1},{2,3},{4,5},{6,7},{8,9},{10,11},{12,13},{14,15},{16,17},{18,... | collective-permute-start | bytes 147464 | tf_op jit(solution)/shard_map/ppermute | solution.py:17
  120.3 0.8 collective-permute-done.9
  121.6 2.7 %collective-permute-start.10 = (f32[3,16,512]{2,1,0:T(8,128)S(1)}, f32[3,16,512]{2,1,0:T(8,128)S(1)}, u32[]{:S(2)}, u32[]{:S(2)}) collective-permute-start(f32[3,16,512]{2,1,0:T(8,128)S(1)} %pad_maximum_fusion.2), channel_id=1, source_target_pairs={{0,2},{2,0},{4,6},{6,4},{8,10},{10,8},{12,14},{14,12},{1,3},{3,1},... | collective-permute-start | bytes 294920 | tf_op jit(solution)/shard_map/ppermute | solution.py:205
  124.3 3.3 %collective-permute-done.10 = f32[3,16,512]{2,1,0:T(8,128)S(1)} collective-permute-done((f32[3,16,512]{2,1,0:T(8,128)S(1)}, f32[3,16,512]{2,1,0:T(8,128)S(1)}, u32[]{:S(2)}, u32[]{:S(2)}) %collective-permute-start.10) | collective-permute-done | bytes 98336 | tf_op jit(solution)/shard_map/ppermute | solution.py:205
  127.7 1.6 %collective-permute-start.11 = (f32[3,16,512]{2,1,0:T(8,128)S(1)}, f32[3,16,512]{2,1,0:T(8,128)S(1)}, u32[]{:S(2)}, u32[]{:S(2)}) collective-permute-start(f32[3,16,512]{2,1,0:T(8,128)S(1)} %pad_maximum_fusion.3), channel_id=1, source_target_pairs={{0,4},{2,6},{4,0},{6,2},{8,12},{10,14},{12,8},{14,10},{1,5},{3,7},... | collective-permute-start | bytes 294920 | tf_op jit(solution)/shard_map/ppermute | solution.py:205
  129.3 3.0 %collective-permute-done.11 = f32[3,16,512]{2,1,0:T(8,128)S(1)} collective-permute-done((f32[3,16,512]{2,1,0:T(8,128)S(1)}, f32[3,16,512]{2,1,0:T(8,128)S(1)}, u32[]{:S(2)}, u32[]{:S(2)}) %collective-permute-start.11) | collective-permute-done | bytes 98336 | tf_op jit(solution)/shard_map/ppermute | solution.py:205
  132.4 2.6 %collective-permute-start.12 = (f32[3,16,512]{2,1,0:T(8,128)S(1)}, f32[3,16,512]{2,1,0:T(8,128)S(1)}, u32[]{:S(2)}, u32[]{:S(2)}) collective-permute-start(f32[3,16,512]{2,1,0:T(8,128)S(1)} %pad_maximum_fusion.4), channel_id=1, source_target_pairs={{0,8},{2,10},{4,12},{6,14},{8,0},{10,2},{12,4},{14,6},{1,9},{3,11}... | collective-permute-start | bytes 294920 | tf_op jit(solution)/shard_map/ppermute | solution.py:205
  135.0 3.0 %collective-permute-done.12 = f32[3,16,512]{2,1,0:T(8,128)S(1)} collective-permute-done((f32[3,16,512]{2,1,0:T(8,128)S(1)}, f32[3,16,512]{2,1,0:T(8,128)S(1)}, u32[]{:S(2)}, u32[]{:S(2)}) %collective-permute-start.12) | collective-permute-done | bytes 98336 | tf_op jit(solution)/shard_map/ppermute | solution.py:205
  (56 shorter events, 4.0 us)
Async XLA Ops:
  0.0 1.3 copy-start
  0.0 1.5 %copy-start.1 = (bf16[27,32,32]{2,1,0:T(8,128)(2,1)S(1)}, bf16[27,32,32]{2,1,0:T(8,128)(2,1)}, u32[]{:S(2)}) copy-start(bf16[27,32,32]{2,1,0:T(8,128)(2,1)} %param.13) | copy-start | bytes 165892
  11.4 12.4 %copy-start.2 = (f32[32]{0:T(128)S(1)}, f32[32]{0:T(128)}, u32[]{:S(2)}) copy-start(f32[32]{0:T(128)} %param.14) | copy-start | bytes 388
  11.4 12.6 %collective-permute-start.2 = (bf16[24,32,512]{2,1,0:T(8,128)(2,1)}, bf16[24,32,512]{2,1,0:T(8,128)(2,1)}, u32[]{:S(2)}, u32[]{:S(2)}) collective-permute-start(bf16[24,32,512]{2,1,0:T(8,128)(2,1)} %get-tuple-element.58), channel_id=1, source_target_pairs={{0,1},{2,3},{4,5},{6,7},{8,9},{10,11},{12,13},{14,15},{16,17},{18,... | collective-permute-start | bytes 2359304 | tf_op jit(solution)/shard_map/ppermute | solution.py:17
  14.9 10.0 %collective-permute-start.3 = (bf16[24,32,512]{2,1,0:T(8,128)(2,1)}, bf16[24,32,512]{2,1,0:T(8,128)(2,1)}, u32[]{:S(2)}, u32[]{:S(2)}) collective-permute-start(bf16[24,32,512]{2,1,0:T(8,128)(2,1)} %get-tuple-element.60), channel_id=1, source_target_pairs={{1,0},{3,2},{5,4},{7,6},{9,8},{11,10},{13,12},{15,14},{17,16},{19,... | collective-permute-start | bytes 2359304 | tf_op jit(solution)/shard_map/ppermute | solution.py:17
  18.2 74.2 %collective-permute-start = (bf16[32,16,512]{2,1,0:T(8,128)(2,1)}, bf16[32,16,512]{2,1,0:T(8,128)(2,1)S(1)}, u32[]{:S(2)}, u32[]{:S(2)}) collective-permute-start(bf16[32,16,512]{2,1,0:T(8,128)(2,1)} %get-tuple-element.68), channel_id=1, source_target_pairs={{0,2},{2,4},{4,6},{6,8},{8,10},{10,12},{12,14},{1,3},{3,5},{5,7},{... | collective-permute-start | bytes 1572872 | tf_op jit(solution)/shard_map/ppermute | solution.py:17
  22.5 70.0 %collective-permute-start.1 = (bf16[32,16,512]{2,1,0:T(8,128)(2,1)S(1)}, bf16[32,16,512]{2,1,0:T(8,128)(2,1)S(1)}, u32[]{:S(2)}, u32[]{:S(2)}) collective-permute-start(bf16[32,16,512]{2,1,0:T(8,128)(2,1)S(1)} %get-tuple-element.67), channel_id=1, source_target_pairs={{2,0},{4,2},{6,4},{8,6},{10,8},{12,10},{14,12},{3,1},{5,3},{7,5},{... | collective-permute-start | bytes 1572872 | tf_op jit(solution)/shard_map/ppermute | solution.py:17
  25.7 66.6 %collective-permute-start.4 = (bf16[128,512]{1,0:T(8,128)(2,1)S(1)}, bf16[128,512]{1,0:T(8,128)(2,1)S(1)}, u32[]{:S(2)}, u32[]{:S(2)}) collective-permute-start(bf16[128,512]{1,0:T(8,128)(2,1)S(1)} %pad_maximum_fusion), channel_id=1, source_target_pairs={{0,2},{2,4},{4,6},{6,8},{8,10},{10,12},{12,14},{1,3},{3,5},{5,7},{... | collective-permute-start | bytes 393224 | tf_op jit(solution)/shard_map/ppermute | solution.py:17
  30.3 62.2 %collective-permute-start.5 = (bf16[128,512]{1,0:T(8,128)(2,1)S(1)}, bf16[128,512]{1,0:T(8,128)(2,1)S(1)}, u32[]{:S(2)}, u32[]{:S(2)}) collective-permute-start(bf16[128,512]{1,0:T(8,128)(2,1)S(1)} %pad_maximum_fusion.1), channel_id=1, source_target_pairs={{2,0},{4,2},{6,4},{8,6},{10,8},{12,10},{14,12},{3,1},{5,3},{7,5},{... | collective-permute-start | bytes 393224 | tf_op jit(solution)/shard_map/ppermute | solution.py:17
  102.9 6.7 %collective-permute-start.6 = (f32[24,512]{1,0:T(8,128)S(1)}, f32[24,512]{1,0:T(8,128)S(1)}, u32[]{:S(2)}, u32[]{:S(2)}) collective-permute-start(f32[24,512]{1,0:T(8,128)S(1)} %get-tuple-element.74), channel_id=1, source_target_pairs={{0,2},{2,4},{4,6},{6,8},{8,10},{10,12},{12,14},{1,3},{3,5},{5,7},{... | collective-permute-start | bytes 147464 | tf_op jit(solution)/shard_map/ppermute | solution.py:17
  107.9 7.3 %collective-permute-start.7 = (f32[24,512]{1,0:T(8,128)S(1)}, f32[24,512]{1,0:T(8,128)S(1)}, u32[]{:S(2)}, u32[]{:S(2)}) collective-permute-start(f32[24,512]{1,0:T(8,128)S(1)} %get-tuple-element.73), channel_id=1, source_target_pairs={{2,0},{4,2},{6,4},{8,6},{10,8},{12,10},{14,12},{3,1},{5,3},{7,5},{... | collective-permute-start | bytes 147464 | tf_op jit(solution)/shard_map/ppermute | solution.py:17
  115.4 4.9 %collective-permute-start.8 = (f32[24,512]{1,0:T(8,128)S(1)}, f32[24,512]{1,0:T(8,128)S(1)}, u32[]{:S(2)}, u32[]{:S(2)}) collective-permute-start(f32[24,512]{1,0:T(8,128)S(1)} %bitcast.182), channel_id=1, source_target_pairs={{1,0},{3,2},{5,4},{7,6},{9,8},{11,10},{13,12},{15,14},{17,16},{19,... | collective-permute-start | bytes 147464 | tf_op jit(solution)/shard_map/ppermute | solution.py:17
  117.2 3.9 %collective-permute-start.9 = (f32[24,512]{1,0:T(8,128)S(1)}, f32[24,512]{1,0:T(8,128)S(1)}, u32[]{:S(2)}, u32[]{:S(2)}) collective-permute-start(f32[24,512]{1,0:T(8,128)S(1)} %bitcast.183), channel_id=1, source_target_pairs={{0,1},{2,3},{4,5},{6,7},{8,9},{10,11},{12,13},{14,15},{16,17},{18,... | collective-permute-start | bytes 147464 | tf_op jit(solution)/shard_map/ppermute | solution.py:17
  121.6 6.0 %collective-permute-start.10 = (f32[3,16,512]{2,1,0:T(8,128)S(1)}, f32[3,16,512]{2,1,0:T(8,128)S(1)}, u32[]{:S(2)}, u32[]{:S(2)}) collective-permute-start(f32[3,16,512]{2,1,0:T(8,128)S(1)} %pad_maximum_fusion.2), channel_id=1, source_target_pairs={{0,2},{2,0},{4,6},{6,4},{8,10},{10,8},{12,14},{14,12},{1,3},{3,1},... | collective-permute-start | bytes 294920 | tf_op jit(solution)/shard_map/ppermute | solution.py:205
  127.7 4.7 %collective-permute-start.11 = (f32[3,16,512]{2,1,0:T(8,128)S(1)}, f32[3,16,512]{2,1,0:T(8,128)S(1)}, u32[]{:S(2)}, u32[]{:S(2)}) collective-permute-start(f32[3,16,512]{2,1,0:T(8,128)S(1)} %pad_maximum_fusion.3), channel_id=1, source_target_pairs={{0,4},{2,6},{4,0},{6,2},{8,12},{10,14},{12,8},{14,10},{1,5},{3,7},... | collective-permute-start | bytes 294920 | tf_op jit(solution)/shard_map/ppermute | solution.py:205
  132.4 5.6 %collective-permute-start.12 = (f32[3,16,512]{2,1,0:T(8,128)S(1)}, f32[3,16,512]{2,1,0:T(8,128)S(1)}, u32[]{:S(2)}, u32[]{:S(2)}) collective-permute-start(f32[3,16,512]{2,1,0:T(8,128)S(1)} %pad_maximum_fusion.4), channel_id=1, source_target_pairs={{0,8},{2,10},{4,12},{6,14},{8,0},{10,2},{12,4},{14,6},{1,9},{3,11}... | collective-permute-start | bytes 294920 | tf_op jit(solution)/shard_map/ppermute | solution.py:205

commit v3 on v2

--- a/solution.py
+++ b/solution.py
@@ -9,6 +9,7 @@
 
 BF = jnp.bfloat16
 F32 = jnp.float32
+MESH = pl.DeviceIdType.MESH
 
 
 def shifted(x, axis, step):
@@ -208,6 +209,149 @@
     return value
 
 
+def finish_kernel(planes, cost, out, work, slab, prev, following, stats, taken, final, one, each):
+    n = lax.axis_size("disp")
+    me = lax.axis_index("disp")
+    r = lax.axis_index("rows")
+    height, width = out.shape
+    across = width // 128
+
+    barrier = pltpu.get_barrier_semaphore()
+    pl.semaphore_signal(barrier, inc=1, device_id={"rows": 1 - r}, device_id_type=MESH)
+    for j in range(1, n):
+        pl.semaphore_signal(barrier, inc=1, device_id={"disp": lax.rem(me + j, n)}, device_id_type=MESH)
+    pl.semaphore_wait(barrier, n)
+
+    def send(src, dst, sems, index, where):
+        return pltpu.make_async_remote_copy(
+            src_ref=src,
+            dst_ref=dst,
+            send_sem=sems.at[0, index],
+            recv_sem=sems.at[1, index],
+            device_id=where,
+            device_id_type=MESH,
+        )
+
+    swap = send(cost.at[:, height : height + 8, :], slab, one, 0, {"rows": 1 - r})
+    swap.start()
+    work[...] = cost[:, :height, :]
+    swap.wait()
+    row = lax.broadcasted_iota(jnp.int32, (height, width), 0)
+    mine = row == (1 - r) * (height - 1)
+    for p in (0, planes + 1):
+        line = jnp.broadcast_to(slab[p, pl.ds(r, 1), :], (height, width))
+        work[p] += jnp.where(mine, line, 0.0)
+
+    up = send(work.at[planes + 1], prev, one, 1, {"disp": jnp.minimum(me + 1, n - 1)})
+    down = send(work.at[0], following, one, 2, {"disp": jnp.maximum(me - 1, 0)})
+
+    @pl.when(me < n - 1)
+    def _():
+        up.start()
+
+    @pl.when(me > 0)
+    def _():
+        down.start()
+
+    for p in range(1, planes + 1):
+        line = jnp.broadcast_to(slab[p, pl.ds(r, 1), :], (height, width))
+        work[p] += jnp.where(mine, line, 0.0)
+
+    @pl.when(me < n - 1)
+    def _():
+        up.wait_send()
+        down.wait_recv()
+
+    @pl.when(me > 0)
+    def _():
+        down.wait_send()
+        up.wait_recv()
+
+    @pl.when(me > 0)
+    def _():
+        work[1] += prev[...]
+
+    @pl.when(me < n - 1)
+    def _():
+        work[planes] += following[...]
+
+    low = work[1]
+    for p in range(2, planes + 1):
+        low = jnp.minimum(low, work[p])
+    base = (me * planes).astype(F32)
+    total = jnp.zeros((height, width), F32)
+    moment = jnp.zeros((height, width), F32)
+    for p in range(planes):
+        expo = jnp.exp(low - work[p + 1])
+        total += expo
+        moment += (base + float(p)) * expo
+    peak = -low
+
+    def place(k):
+        at = (k // across) * 8, (k % across) * 128
+        return slice(at[0], at[0] + 8), slice(at[1], at[1] + 128)
+
+    for k in range(n):
+        rows, cols = place(k)
+        stats[k, 0] = peak[rows, cols]
+        stats[k, 1] = total[rows, cols]
+        stats[k, 2] = moment[rows, cols]
+
+    copies = []
+    for j in range(1, n):
+        peer = lax.rem(me + j, n)
+        copies.append(send(stats.at[peer], taken.at[j], each, j, {"disp": peer}))
+        copies[-1].start()
+    for copy in copies:
+        copy.wait()
+    parts = [stats[me]] + [taken[j] for j in range(1, n)]
+    top = parts[0][0]
+    for part in parts[1:]:
+        top = jnp.maximum(top, part[0])
+    total = jnp.zeros_like(top)
+    moment = jnp.zeros_like(top)
+    for part in parts:
+        scale = jnp.exp(part[0] - top)
+        total += part[1] * scale
+        moment += part[2] * scale
+    final[me] = moment / total
+
+    copies = []
+    for j in range(1, n):
+        peer = lax.rem(me + j, n)
+        copies.append(send(final.at[me], final.at[me], each, n + j, {"disp": peer}))
+        copies[-1].start()
+    for copy in copies:
+        copy.wait()
+    for k in range(n):
+        rows, cols = place(k)
+        out[rows, cols] = final[k]
+
+
+def finish(cost, height):
+    planes, width = cost.shape[0] - 2, cost.shape[2]
+    n = lax.axis_size("disp")
+    return pl.pallas_call(
+        functools.partial(finish_kernel, planes),
+        in_specs=[pl.BlockSpec(memory_space=pltpu.VMEM)],
+        out_specs=pl.BlockSpec(memory_space=pltpu.VMEM),
+        out_shape=jax.ShapeDtypeStruct((height, width), F32),
+        scratch_shapes=[
+            pltpu.VMEM((planes + 2, height, width), F32),
+            pltpu.VMEM((planes + 2, 8, width), F32),
+            pltpu.VMEM((height, width), F32),
+            pltpu.VMEM((height, width), F32),
+            pltpu.VMEM((n, 3, 8, 128), F32),
+            pltpu.VMEM((n, 3, 8, 128), F32),
+            pltpu.VMEM((n, 8, 128), F32),
+            pltpu.SemaphoreType.DMA((2, 3)),
+            pltpu.SemaphoreType.DMA((2, 2 * n)),
+        ],
+        compiler_params=pltpu.CompilerParams(collective_id=0, has_side_effects=True),
+        name="finish",
+    )(cost)
+
+
 def body(volume, conv_weight, conv_bias, reg_weight):
     ch, planes, height, width = volume.shape
     half = height // 2
@@ -220,9 +364,6 @@
 
     def shape(*dims, dtype=BF):
         return jax.ShapeDtypeStruct(dims, dtype)
-
-    before = shifted(volume[:, planes - 1], "disp", 1)
-    after = shifted(volume[:, 0], "disp", -1)
 
     wide = spread(conv_weight, half)
     taps = jnp.transpose(conv_weight.reshape(3, 3, 3, ch, ch)[:, ::2], (0, 3, 2, 1, 4)).reshape(3, ch, 6 * ch)
@@ -268,9 +409,13 @@
     def edges(p):
         return jnp.concatenate([above[p], local[p], below[p]], axis=0)
 
-    head, foot = edges(0), edges(planes - 1)
-    edge_before = shifted(foot, "disp", 1)
-    edge_after = shifted(head, "disp", -1)
+    def packed(p):
+        return jnp.concatenate([volume[:, p], edges(p).reshape(4 * ch // height, height, width)], axis=0)
+
+    before = shifted(packed(planes - 1), "disp", 1)
+    after = shifted(packed(0), "disp", -1)
+    edge_before = before[ch:].reshape(4 * ch, width)
+    edge_after = after[ch:].reshape(4 * ch, width)
 
     cost_shape = shape(planes + 2, rows, width, dtype=F32)
     cost_spec = pl.BlockSpec(cost_shape.shape, lambda i: (0, 0, 0))
@@ -304,7 +449,9 @@
     def rim_plane(i):
         return jnp.where(i < 3, jnp.maximum(i - 1, 0), jnp.minimum(planes + i - 5, planes - 1))
 
-    rim_e = jnp.stack([edge_before, head, edges(1), edges(planes - 2), foot, edge_after])
+    rim_e = jnp.stack(
+        [edge_before, edges(0), edges(1), edges(planes - 2), edges(planes - 1), edge_after]
+    )
     cost = pl.pallas_call(
         functools.partial(rim_kernel, planes),
         grid=(6,),
@@ -329,6 +476,10 @@
         name="rim",
     )(volume, volume, before, before, after, after, rim_e, a, bias, r, cost)
 
+    n = lax.axis_size("disp")
+    if lax.axis_size("rows") == 2 and height % 8 == 0 and height * width == 1024 * n:
+        return finish(cost, height)
+
     from_before = shifted(cost[planes + 1], "disp", 1)
     from_after = shifted(cost[0], "disp", -1)
     cost = cost[1 : planes + 1]

time: 139 us -> 120 us (0.86)
  starting transfers between devices: 33.6 us -> 9.92 us
  Pallas kernels: 80.8 us -> 101 us
  waiting for transfers between devices: 16.2 us -> 1.57 us
    pallas_call x0 -> x1, Pallas kernels: none -> 20.7 us  [finish(): pl.pallas_call(functools.partial(finish_kernel, planes), in_specs=[pl.Blo...]
    ppermute x10 -> x4, starting transfers between devices: 26.6 us -> 9.92 us  [shifted(): return lax.ppermute(x, axis, pairs)]
    ppermute x3 -> x0, waiting for transfers between devices: 9.31 us -> none  [joined(): other = lax.ppermute(value, axis, [(i, i ^ step) for i in range(count)])]
    ppermute x3 -> x0, starting transfers between devices: 6.97 us -> none  [joined(): other = lax.ppermute(value, axis, [(i, i ^ step) for i in range(count)])]
    ppermute x10 -> x4, waiting for transfers between devices: 6.87 us -> 1.57 us  [shifted(): return lax.ppermute(x, axis, pairs)]
    unnamed x13, local copies, waits for them, and re-layouts: 0.64 us -> 3.31 us
    squeeze x3, local copies, waits for them, and re-layouts: 1.66 us -> 0.04 us  [edges(): return jnp.concatenate([above[p], local[p], below[p]], axis=0)]
  transfers between devices with their start and end apart: 13 -> 4, of which waited for: 6 -> 1; matrix products, arithmetic and copies ran while one was open for 3% -> 1% of each run, Pallas kernels for 44% -> 51%
where the time goes in v3:
time: 120 us; the launch traced here: 119 us
  Pallas kernels  101 us (84%)
  starting transfers between devices  9.92 us (8%)
  local copies, waits for them, and re-layouts  5 us (4%)
  waiting for transfers between devices  1.57 us (1%)
  matrix products  1.31 us (1%)
    pallas_call x1, Pallas kernels, body(): pl.pallas_call(inner_kernel, grid=(planes,), in_specs=[pl.BlockSpec((ch,...  60.4 us
    pallas_call x1, Pallas kernels, finish(): pl.pallas_call(functools.partial(finish_kernel, planes), in_specs=[pl.Blo...  20.7 us
    pallas_call x1, Pallas kernels, body(): pl.pallas_call(functools.partial(rim_kernel, planes), grid=(6,), in_specs...  10.4 us
    ppermute x4, starting transfers between devices, shifted(): return lax.ppermute(x, axis, pairs)  9.92 us
    pallas_call x1, Pallas kernels, body(): pl.pallas_call(prep_kernel, grid=(planes // group,), in_specs=[pl.BlockSp...  9.62 us
    unnamed x13, local copies, waits for them, and re-layouts  3.31 us
  transfers between devices with their start and end apart: 4, of which 1 were waited for; matrix products, arithmetic and copies ran while one was open for 1% of the time, Pallas kernels for 51%

profile of v3, /device:TPU:0, one launch (start us, length us, event | category | flops | bytes accessed | tf_op | source)
XLA Modules:
  0.0 119.4 jit_solution(5897725414511120265)
XLA Ops:
  0.0 0.7 copy-done
  0.7 0.1 convolution_bitcast_fusion.1
  0.9 1.2 convolution_bitcast_fusion.wide
  2.1 0.1 copy.18
  2.2 0.1 reshape.54
  2.4 0.0 copy-start.3
  2.4 9.6 %prep.1 = (bf16[24,32,512]{2,1,0:T(8,128)(2,1)}, bf16[24,32,512]{2,1,0:T(8,128)(2,1)}, bf16[24,64,512]{2,1,0:T(8,128)(2,1)S(1)}, bf16[256,5120]{1,0:T(8,128)(2,1)}, bf16[216,512]{1,0:T(8,128)(2,1)S(1)}) custom-call(bf16[32,24,16,512]{3,2,1,0:T(8,128)(2,1)} %hi.3, f32[27,32,256]{2,1,0:T(8,128)S(1)} %convolution_bitcast_fusion.wide, ...), custom_call_target="tpu_custom_call" | custom-call | flops 1610612736 | bytes 12582912 | tf_op jit(solution)/shard_map/prep/pallas_call | solution.py:375
  12.0 2.4 %collective-permute-start = (bf16[24,32,512]{2,1,0:T(8,128)(2,1)}, bf16[24,32,512]{2,1,0:T(8,128)(2,1)S(1)}, u32[]{:S(2)}, u32[]{:S(2)}) collective-permute-start(bf16[24,32,512]{2,1,0:T(8,128)(2,1)} %get-tuple-element.10), channel_id=1, source_target_pairs={{0,1},{2,3},{4,5},{6,7},{8,9},{10,11},{12,13},{14,15},{16,17},{18,... | collective-permute-start | bytes 2359304 | tf_op jit(solution)/shard_map/ppermute | solution.py:18
  14.5 1.3 %collective-permute-start.1 = (bf16[24,32,512]{2,1,0:T(8,128)(2,1)}, bf16[24,32,512]{2,1,0:T(8,128)(2,1)S(1)}, u32[]{:S(2)}, u32[]{:S(2)}) collective-permute-start(bf16[24,32,512]{2,1,0:T(8,128)(2,1)} %get-tuple-element.12), channel_id=1, source_target_pairs={{1,0},{3,2},{5,4},{7,6},{9,8},{11,10},{13,12},{15,14},{17,16},{19,... | collective-permute-start | bytes 2359304 | tf_op jit(solution)/shard_map/ppermute | solution.py:18
  15.8 0.1 broadcast_in_dim.2
  15.9 0.1 broadcast_in_dim_reshape.4.bias
  16.0 1.3 %slice_bitcast_fusion = (bf16[32,16,512]{2,1,0:T(8,128)(2,1)S(1)}, bf16[32,16,512]{2,1,0:T(8,128)(2,1)S(1)}) fusion(bf16[32,24,16,512]{3,2,1,0:T(8,128)(2,1)} %hi.3), kind=kLoop, calls=%fused_computation.4 | loop fusion | bytes 2097152 | tf_op jit(solution)/shard_map/squeeze | solution.py:413
  17.3 0.0 collective-permute-done.above
  17.3 1.6 %collective-permute-done.1.below = bf16[24,32,512]{2,1,0:T(8,128)(2,1)S(1)} collective-permute-done((bf16[24,32,512]{2,1,0:T(8,128)(2,1)}, bf16[24,32,512]{2,1,0:T(8,128)(2,1)S(1)}, u32[]{:S(2)}, u32[]{:S(2)}) %collective-permute-start.1) | collective-permute-done | bytes 786464 | tf_op jit(solution)/shard_map/ppermute | solution.py:18
  18.9 0.1 pad_maximum_fusion.1
  19.0 1.3 %collective-permute-start.3 = (bf16[40,16,512]{2,1,0:T(8,128)(2,1)S(1)}, bf16[40,16,512]{2,1,0:T(8,128)(2,1)S(1)}, u32[]{:S(2)}, u32[]{:S(2)}) collective-permute-start(bf16[40,16,512]{2,1,0:T(8,128)(2,1)S(1)} %pad_maximum_fusion.1), channel_id=1, source_target_pairs={{2,0},{4,2},{6,4},{8,6},{10,8},{12,10},{14,12},{3,1},{5,3},{7,5},{... | collective-permute-start | bytes 1966088 | tf_op jit(solution)/shard_map/ppermute | solution.py:18
  20.3 0.1 pad_maximum_fusion
  20.3 4.9 %collective-permute-start.2 = (bf16[40,16,512]{2,1,0:T(8,128)(2,1)S(1)}, bf16[40,16,512]{2,1,0:T(8,128)(2,1)S(1)}, u32[]{:S(2)}, u32[]{:S(2)}) collective-permute-start(bf16[40,16,512]{2,1,0:T(8,128)(2,1)S(1)} %pad_maximum_fusion), channel_id=1, source_target_pairs={{0,2},{2,4},{4,6},{6,8},{8,10},{10,12},{12,14},{1,3},{3,5},{5,7},{... | collective-permute-start | bytes 1966088 | tf_op jit(solution)/shard_map/ppermute | solution.py:18
  25.2 60.4 %inner.1.cost_in = f32[26,24,512]{2,1,0:T(8,128)S(1)} custom-call(bf16[32,24,16,512]{3,2,1,0:T(8,128)(2,1)} %hi.3, bf16[32,24,16,512]{3,2,1,0:T(8,128)(2,1)} %hi.3, bf16[24,32,512]{2,1,0:T(8,128)(2,1)S(1)} %collective-permute-done.above, bf16[24,64,512]{2,1,0:T(8,128)(2,1)S(1)} %get-tuple-element.11.local, ...), custom_call_target="tpu_custom_call" | custom-call | flops 35433480192 | bytes 12582912 | tf_op jit(solution)/shard_map/inner/pallas_call | solution.py:426
  85.6 0.0 collective-permute-done.2.b_lo.b_hi
  85.8 10.4 %rim.1.cost = f32[26,24,512]{2,1,0:T(8,128)S(1)} custom-call(bf16[32,24,16,512]{3,2,1,0:T(8,128)(2,1)} %hi.3, bf16[32,24,16,512]{3,2,1,0:T(8,128)(2,1)} %hi.3, bf16[40,16,512]{2,1,0:T(8,128)(2,1)S(1)} %collective-permute-done.2.b_lo.b_hi, bf16[40,16,512]{2,1,0:T(8,128)(2,1)S(1)} %collective-permute-done.2.b_lo.b_hi, ...), custom_call_target="tpu_custom_call" | custom-call | flops 3221225472 | bytes 3145728 | tf_op jit(solution)/shard_map/rim/pallas_call | solution.py:455
  96.2 1.1 copy-done.1
  97.3 20.7 %finish.1 = f32[16,512]{1,0:T(8,128)} custom-call(f32[26,24,512]{2,1,0:T(8,128)} %copy-done.1), custom_call_target="tpu_custom_call" | custom-call | tf_op jit(solution)/shard_map/finish/pallas_call | solution.py:334
  118.0 1.4 %copy.25 = f32[16,512]{1,0:T(8,128)} copy(f32[16,512]{1,0:T(8,128)} %finish.1) | data formatting | bytes 65536
  (24 shorter events, 0.2 us)
Async XLA Ops:
  0.0 0.7 copy-start
  0.0 2.1 %copy-start.2 = (bf16[27,32,32]{2,1,0:T(8,128)(2,1)S(1)}, bf16[27,32,32]{2,1,0:T(8,128)(2,1)}, u32[]{:S(2)}) copy-start(bf16[27,32,32]{2,1,0:T(8,128)(2,1)} %param.5) | copy-start | bytes 165892
  2.4 13.4 %copy-start.3 = (f32[32]{0:T(128)S(1)}, f32[32]{0:T(128)}, u32[]{:S(2)}) copy-start(f32[32]{0:T(128)} %param.6) | copy-start | bytes 388
  12.0 5.2 %collective-permute-start = (bf16[24,32,512]{2,1,0:T(8,128)(2,1)}, bf16[24,32,512]{2,1,0:T(8,128)(2,1)S(1)}, u32[]{:S(2)}, u32[]{:S(2)}) collective-permute-start(bf16[24,32,512]{2,1,0:T(8,128)(2,1)} %get-tuple-element.10), channel_id=1, source_target_pairs={{0,1},{2,3},{4,5},{6,7},{8,9},{10,11},{12,13},{14,15},{16,17},{18,... | collective-permute-start | bytes 2359304 | tf_op jit(solution)/shard_map/ppermute | solution.py:18
  14.5 4.4 %collective-permute-start.1 = (bf16[24,32,512]{2,1,0:T(8,128)(2,1)}, bf16[24,32,512]{2,1,0:T(8,128)(2,1)S(1)}, u32[]{:S(2)}, u32[]{:S(2)}) collective-permute-start(bf16[24,32,512]{2,1,0:T(8,128)(2,1)} %get-tuple-element.12), channel_id=1, source_target_pairs={{1,0},{3,2},{5,4},{7,6},{9,8},{11,10},{13,12},{15,14},{17,16},{19,... | collective-permute-start | bytes 2359304 | tf_op jit(solution)/shard_map/ppermute | solution.py:18
  19.0 66.8 %collective-permute-start.3 = (bf16[40,16,512]{2,1,0:T(8,128)(2,1)S(1)}, bf16[40,16,512]{2,1,0:T(8,128)(2,1)S(1)}, u32[]{:S(2)}, u32[]{:S(2)}) collective-permute-start(bf16[40,16,512]{2,1,0:T(8,128)(2,1)S(1)} %pad_maximum_fusion.1), channel_id=1, source_target_pairs={{2,0},{4,2},{6,4},{8,6},{10,8},{12,10},{14,12},{3,1},{5,3},{7,5},{... | collective-permute-start | bytes 1966088 | tf_op jit(solution)/shard_map/ppermute | solution.py:18
  20.3 65.3 %collective-permute-start.2 = (bf16[40,16,512]{2,1,0:T(8,128)(2,1)S(1)}, bf16[40,16,512]{2,1,0:T(8,128)(2,1)S(1)}, u32[]{:S(2)}, u32[]{:S(2)}) collective-permute-start(bf16[40,16,512]{2,1,0:T(8,128)(2,1)S(1)} %pad_maximum_fusion), channel_id=1, source_target_pairs={{0,2},{2,4},{4,6},{6,8},{8,10},{10,12},{12,14},{1,3},{3,5},{5,7},{... | collective-permute-start | bytes 1966088 | tf_op jit(solution)/shard_map/ppermute | solution.py:18
  96.2 1.1 copy-start.1

commit v4 on v3

--- a/solution.py
+++ b/solution.py
@@ -29,11 +29,11 @@
     return jnp.einsum("...c,cg->...g", rows, onehot, preferred_element_type=F32)
 
 
-def prep_kernel(v_ref, wide, wedge, wreg, last, first, local, a_ref, r_ref, pick):
+def prep_kernel(v_ref, wide, wedge, wreg, last, first, local, a_ref, ae_ref, r_ref, pick):
     ch, count, height, width = v_ref.shape
     half = height // 2
     span = ch * half
-    depth = 3 * span + edge_rows(ch)
+    edge = edge_rows(ch)
 
     @pl.when(pl.program_id(0) == 0)
     def _():
@@ -43,26 +43,24 @@
         at = jnp.where(kind == 0, height - 1, jnp.where(kind == 1, 0, jnp.where(kind == 2, half, half - 1)))
         pick[...] = (col == (row % ch) * height + at).astype(F32).astype(BF)
 
-        shape = (ch, half, span)
-        diff = lax.broadcasted_iota(jnp.int32, shape, 2) % half - lax.broadcasted_iota(jnp.int32, shape, 1)
-        eshape = (ch, half, edge_rows(ch))
-        side = (lax.broadcasted_iota(jnp.int32, eshape, 2) // ch) % 2
-        keep = lax.broadcasted_iota(jnp.int32, eshape, 1) == side * (half - 1)
+        order = [0, half - 1] + list(range(1, half - 1))
+        at = lax.broadcasted_iota(jnp.int32, (ch, span), 1) % half
+        side = (lax.broadcasted_iota(jnp.int32, (ch, edge), 1) // ch) % 2
         for a in range(3):
             for c in range(3):
-                out = jnp.zeros(shape, F32)
-                for b in range(3):
-                    line = jnp.broadcast_to(wide[9 * a + 3 * b + c][:, None, :], shape)
-                    out = jnp.where(diff == b - 1, line, out)
-                block = out.reshape(span, span).astype(BF)
-                for slot in (a, a + 3):
-                    if slot < 5:
-                        a_ref[:, slot * depth + c * span : slot * depth + (c + 1) * span] = block
-            line = jnp.broadcast_to(wedge[a][:, None, :], eshape)
-            block = jnp.where(keep, line, 0.0).reshape(span, edge_rows(ch)).astype(BF)
-            for slot in (a, a + 3):
-                if slot < 5:
-                    a_ref[:, slot * depth + 3 * span : (slot + 1) * depth] = block
+                lines = [wide[9 * a + 3 * b + c] for b in range(3)]
+                for k, h in enumerate(order):
+                    out = jnp.zeros((ch, span), F32)
+                    for b in range(3):
+                        out = jnp.where(at == h + b - 1, lines[b], out)
+                    out = out.astype(BF)
+                    for slot in range(a, 5, 3):
+                        base = slot * 3 * span + c * span
+                        a_ref[k * ch : (k + 1) * ch, base : base + span] = out
+            for k in range(2):
+                out = jnp.where(side == k, wedge[a], 0.0).astype(BF)
+                for slot in range(a, 5, 3):
+                    ae_ref[k * ch : (k + 1) * ch, slot * edge : (slot + 1) * edge] = out
 
         rshape = (height + 8, 2 * span)
         row = lax.broadcasted_iota(jnp.int32, rshape, 0)
@@ -70,7 +68,9 @@
         place = jnp.where(
             row < height, row, jnp.where(row == height, -1, jnp.where(row == height + 1, height, -9))
         )
-        diff = (col // span) * half + col % half - place
+        turn = (col % span) // ch
+        inside = jnp.where(turn == 0, 0, jnp.where(turn == 1, half - 1, turn - 1))
+        diff = (col // span) * half + inside - place
         blocks = []
         for a in range(3):
             for c in range(3):
@@ -100,27 +100,32 @@
     return move(x.astype(F32), step).astype(BF) if step else x
 
 
-def put_half(x3, slot, x, top, bottom):
+def put_half(x3, xe, slot, x, top, bottom):
     span, ch = x.shape[0], top.shape[0]
-    depth = x3.shape[1]
+    edge = xe.shape[1]
     for k, step in enumerate((1, 0, -1)):
         x3[slot, k * span : (k + 1) * span, :] = moved(x, step)
-        base = 3 * span + 2 * k * ch
-        x3[slot, base : base + ch, :] = moved(top, step)
-        x3[slot, base + ch : base + 2 * ch, :] = moved(bottom, step)
-    tail = 3 * span + 6 * ch
-    if tail < depth:
-        x3[slot, tail:depth, :] = jnp.zeros((depth - tail, x.shape[1]), BF)
-
-
-def out_plane(phase, a_ref, halves, bias, r_ref, cost, at):
-    slots, depth, width = halves[0].shape
-    start = phase * depth if isinstance(phase, int) else pl.multiple_of(phase * depth, 128)
+        base = 2 * k * ch
+        xe[slot, base : base + ch, :] = moved(top, step)
+        xe[slot, base + ch : base + 2 * ch, :] = moved(bottom, step)
+    if 6 * ch < edge:
+        xe[slot, 6 * ch : edge, :] = jnp.zeros((edge - 6 * ch, x.shape[1]), BF)
+
+
+def out_plane(phase, a_ref, ae_ref, halves, bias, r_ref, cost, at):
+    def product(matrix, x3):
+        slots, depth, width = x3.shape
+        start = phase * depth if isinstance(phase, int) else pl.multiple_of(phase * depth, 128)
+        x = x3[...].reshape(slots * depth, width)
+        return jnp.dot(matrix[:, pl.ds(start, slots * depth)], x, preferred_element_type=F32)
+
     hidden = []
-    for x3 in halves:
-        a = a_ref[:, pl.ds(start, slots * depth)]
-        acc = jnp.dot(a, x3[...].reshape(slots * depth, width), preferred_element_type=F32)
-        hidden.append(jnp.maximum(acc + bias[...], 0.0).astype(BF))
+    for x3, xe in halves:
+        acc = product(a_ref, x3) + bias[...]
+        extra = product(ae_ref, xe)
+        count = extra.shape[0]
+        hidden.append(jnp.maximum(acc[:count] + extra, 0.0).astype(BF))
+        hidden.append(jnp.maximum(acc[count:], 0.0).astype(BF))
     part = jnp.dot(r_ref[...], jnp.concatenate(hidden, axis=0), preferred_element_type=F32)
     rows = cost.shape[1]
     for tap in range(3):
@@ -137,7 +142,7 @@
     return x.reshape(x.shape[0] * x.shape[1], x.shape[2])
 
 
-def inner_kernel(lo, hi, above, local, below, a_ref, bias, r_ref, cost, x_lo, x_hi):
+def inner_kernel(lo, hi, above, local, below, a_ref, ae_ref, bias, r_ref, cost, x_lo, x_hi, e_lo, e_hi):
     step = pl.program_id(0)
     ch = above.shape[1]
 
@@ -146,16 +151,16 @@
         cost[...] = jnp.zeros_like(cost)
 
     slot = lax.rem(step, 3)
-    put_half(x_lo, slot, flat(lo[:, 0]), above[0], local[0, :ch])
-    put_half(x_hi, slot, flat(hi[:, 0]), local[0, ch:], below[0])
+    put_half(x_lo, e_lo, slot, flat(lo[:, 0]), above[0], local[0, :ch])
+    put_half(x_hi, e_hi, slot, flat(hi[:, 0]), local[0, ch:], below[0])
 
     @pl.when(step >= 2)
     def _():
         first = lax.rem(step + 1, 3)
-        out_plane(lax.rem(3 - first, 3), a_ref, (x_lo, x_hi), bias, r_ref, cost, step - 1)
-
-
-def rim_kernel(planes, lo, hi, b_lo, b_hi, a_lo, a_hi, e_ref, a_ref, bias, r_ref, cost_in, cost, x_lo, x_hi):
+        out_plane(lax.rem(3 - first, 3), a_ref, ae_ref, ((x_lo, e_lo), (x_hi, e_hi)), bias, r_ref, cost, step - 1)
+
+
+def rim_kernel(planes, lo, hi, b_lo, b_hi, a_lo, a_hi, e_ref, a_ref, ae_ref, bias, r_ref, cost_in, cost, x_lo, x_hi, e_lo, e_hi):
     step = pl.program_id(0)
     ch = lo.shape[0]
 
@@ -166,8 +171,8 @@
     slot = lax.rem(step, 3)
 
     def put(low, high):
-        put_half(x_lo, slot, flat(low), e_ref[0, :ch], e_ref[0, ch : 2 * ch])
-        put_half(x_hi, slot, flat(high), e_ref[0, 2 * ch : 3 * ch], e_ref[0, 3 * ch :])
+        put_half(x_lo, e_lo, slot, flat(low), e_ref[0, :ch], e_ref[0, ch : 2 * ch])
+        put_half(x_hi, e_hi, slot, flat(high), e_ref[0, 2 * ch : 3 * ch], e_ref[0, 3 * ch :])
 
     @pl.when(step == 0)
     def _():
@@ -183,7 +188,7 @@
 
     @pl.when(slot == 2)
     def _():
-        out_plane(0, a_ref, (x_lo, x_hi), bias, r_ref, cost, jnp.where(step == 2, 0, planes - 1))
+        out_plane(0, a_ref, ae_ref, ((x_lo, e_lo), (x_hi, e_hi)), bias, r_ref, cost, jnp.where(step == 2, 0, planes - 1))
 
 
 def combine(first, second):
@@ -357,7 +362,8 @@
     half = height // 2
     span = ch * half
     rows = height + 8
-    depth = 3 * span + edge_rows(ch)
+    edge = edge_rows(ch)
+    depth = 3 * span + edge
 
     def whole(x):
         return pl.BlockSpec(x.shape, lambda i: (0,) * len(x.shape), pipeline_mode=pl.Buffered(1))
@@ -368,11 +374,11 @@
     wide = spread(conv_weight, half)
     taps = jnp.transpose(conv_weight.reshape(3, 3, 3, ch, ch)[:, ::2], (0, 3, 2, 1, 4)).reshape(3, ch, 6 * ch)
     wedge = jnp.pad(taps, ((0, 0), (0, 0), (0, edge_rows(ch) - 6 * ch))).astype(F32)
-    wreg = jnp.tile(spread(reg_weight, half), (1, 2))
-    bias = jnp.repeat(conv_bias, half)[:, None]
+    wreg = jnp.tile(reg_weight.astype(F32), (1, height))
+    bias = jnp.tile(conv_bias, half)[:, None]
 
     group = next(n for n in (4, 3, 2, 1) if planes % n == 0)
-    last, first, local, a, r = pl.pallas_call(
+    last, first, local, a, ae, r = pl.pallas_call(
         prep_kernel,
         grid=(planes // group,),
         in_specs=[
@@ -385,14 +391,16 @@
             pl.BlockSpec((group, ch, width), lambda i: (i, 0, 0)),
             pl.BlockSpec((group, ch, width), lambda i: (i, 0, 0)),
             pl.BlockSpec((group, 2 * ch, width), lambda i: (i, 0, 0)),
-            pl.BlockSpec((span, 5 * depth), lambda i: (0, 0)),
+            pl.BlockSpec((span, 15 * span), lambda i: (0, 0)),
+            pl.BlockSpec((2 * ch, 5 * edge), lambda i: (0, 0)),
             pl.BlockSpec((9 * rows, 2 * span), lambda i: (0, 0)),
         ],
         out_shape=[
             shape(planes, ch, width),
             shape(planes, ch, width),
             shape(planes, 2 * ch, width),
-            shape(span, 5 * depth),
+            shape(span, 15 * span),
+            shape(2 * ch, 5 * edge),
             shape(9 * rows, 2 * span),
         ],
         scratch_shapes=[pltpu.VMEM((4 * ch, ch * height), BF)],
@@ -419,7 +427,7 @@
 
     cost_shape = shape(planes + 2, rows, width, dtype=F32)
     cost_spec = pl.BlockSpec(cost_shape.shape, lambda i: (0, 0, 0))
-    scratch = [pltpu.VMEM((3, depth, width), BF)] * 2
+    scratch = [pltpu.VMEM((3, 3 * span, width), BF)] * 2 + [pltpu.VMEM((3, edge, width), BF)] * 2
     params = pltpu.CompilerParams(vmem_limit_bytes=48 << 20)
     flops = 4 * span * 3 * depth * width
 
@@ -433,6 +441,7 @@
             pl.BlockSpec((1, 2 * ch, width), lambda i: (i, 0, 0)),
             pl.BlockSpec((1, ch, width), lambda i: (i, 0, 0)),
             whole(a),
+            whole(ae),
             whole(bias),
             whole(r),
         ],
@@ -444,7 +453,7 @@
             flops=(planes - 2) * flops, bytes_accessed=2 * volume.size, transcendentals=0
         ),
         name="inner",
-    )(volume, volume, above, local, below, a, bias, r)
+    )(volume, volume, above, local, below, a, ae, bias, r)
 
     def rim_plane(i):
         return jnp.where(i < 3, jnp.maximum(i - 1, 0), jnp.minimum(planes + i - 5, planes - 1))
@@ -464,6 +473,7 @@
             pl.BlockSpec((ch, half, width), lambda i: (0, 1, 0), pipeline_mode=pl.Buffered(1)),
             pl.BlockSpec((1, 4 * ch, width), lambda i: (i, 0, 0)),
             whole(a),
+            whole(ae),
             whole(bias),
             whole(r),
             whole(cost_shape),
@@ -474,7 +484,7 @@
         compiler_params=params,
         cost_estimate=pl.CostEstimate(flops=2 * flops, bytes_accessed=2 * volume.size // 4, transcendentals=0),
         name="rim",
-    )(volume, volume, before, before, after, after, rim_e, a, bias, r, cost)
+    )(volume, volume, before, before, after, after, rim_e, a, ae, bias, r, cost)
 
     n = lax.axis_size("disp")
     if lax.axis_size("rows") == 2 and height % 8 == 0 and height * width == 1024 * n:

time: 120 us -> 117 us (0.975)
  Pallas kernels: 101 us -> 97.1 us
  local copies, waits for them, and re-layouts: 5 us -> 6.86 us
    pallas_call x1, Pallas kernels: 60.4 us -> 57.4 us  [body(): pl.pallas_call(inner_kernel, grid=(planes,), in_specs=[pl.BlockSpec((ch,...]
    unnamed x13 -> x9, local copies, waits for them, and re-layouts: 3.31 us -> 2.59 us
  transfers between devices with their start and end apart: 4 -> 4, of which waited for: 1 -> 1; matrix products, arithmetic and copies ran while one was open for 1% -> 1% of each run, Pallas kernels for 51% -> 49%
where the time goes in v4:
time: 117 us; the launch traced here: 116 us
  Pallas kernels  97.1 us (83%)
  starting transfers between devices  9.92 us (8%)
  local copies, waits for them, and re-layouts  6.86 us (6%)
  waiting for transfers between devices  1.73 us (1%)
    pallas_call x1, Pallas kernels, body(): pl.pallas_call(inner_kernel, grid=(planes,), in_specs=[pl.BlockSpec((ch,...  57.4 us
    pallas_call x1, Pallas kernels, finish(): pl.pallas_call(functools.partial(finish_kernel, planes), in_specs=[pl.Blo...  20.8 us
    pallas_call x1, Pallas kernels, body(): pl.pallas_call(functools.partial(rim_kernel, planes), grid=(6,), in_specs...  9.93 us
    ppermute x4, starting transfers between devices, shifted(): return lax.ppermute(x, axis, pairs)  9.92 us
    pallas_call x1, Pallas kernels, body(): pl.pallas_call(prep_kernel, grid=(planes // group,), in_specs=[pl.BlockSp...  8.98 us
    unnamed x9, local copies, waits for them, and re-layouts  2.59 us
  transfers between devices with their start and end apart: 4, of which 1 were waited for; matrix products, arithmetic and copies ran while one was open for 1% of the time, Pallas kernels for 49%

profile of v4, /device:TPU:0, one launch (start us, length us, event | category | flops | bytes accessed | tf_op | source)
XLA Modules:
  0.0 116.3 jit_solution(16841314783682296442)
XLA Ops:
  0.0 1.0 slice.58
  1.0 0.1 copy.17
  1.1 0.1 reshape.55
  1.3 0.7 tile.6
  2.0 0.1 tile.7.wreg
  2.1 0.3 convolution_bitcast_fusion.wide
  2.4 0.0 copy-start.2
  2.4 9.0 %prep.1 = (bf16[24,32,512]{2,1,0:T(8,128)(2,1)}, bf16[24,32,512]{2,1,0:T(8,128)(2,1)}, bf16[24,64,512]{2,1,0:T(8,128)(2,1)S(1)}, bf16[256,3840]{1,0:T(8,128)(2,1...) custom-call(bf16[32,24,16,512]{3,2,1,0:T(8,128)(2,1)} %hi.3, ...), custom_call_target="tpu_custom_call" | custom-call | flops 1610612736 | bytes 12582912 | tf_op jit(solution)/shard_map/prep/pallas_call | solution.py:381
  11.4 2.4 %collective-permute-start = (bf16[24,32,512]{2,1,0:T(8,128)(2,1)}, bf16[24,32,512]{2,1,0:T(8,128)(2,1)S(1)}, u32[]{:S(2)}, u32[]{:S(2)}) collective-permute-start(bf16[24,32,512]{2,1,0:T(8,128)(2,1)} %get-tuple-element.11), channel_id=1, source_target_pairs={{0,1},{2,3},{4,5},{6,7},{8,9},{10,11},{12,13},{14,15},{16,17},{18,... | collective-permute-start | bytes 2359304 | tf_op jit(solution)/shard_map/ppermute | solution.py:18
  13.8 1.3 %collective-permute-start.1 = (bf16[24,32,512]{2,1,0:T(8,128)(2,1)}, bf16[24,32,512]{2,1,0:T(8,128)(2,1)}, u32[]{:S(2)}, u32[]{:S(2)}) collective-permute-start(bf16[24,32,512]{2,1,0:T(8,128)(2,1)} %get-tuple-element.13), channel_id=1, source_target_pairs={{1,0},{3,2},{5,4},{7,6},{9,8},{11,10},{13,12},{15,14},{17,16},{19,... | collective-permute-start | bytes 2359304 | tf_op jit(solution)/shard_map/ppermute | solution.py:18
  15.1 0.1 broadcast_in_dim_tile.4.bias
  15.3 1.3 %slice_bitcast_fusion = (bf16[32,16,512]{2,1,0:T(8,128)(2,1)S(1)}, bf16[32,16,512]{2,1,0:T(8,128)(2,1)S(1)}) fusion(bf16[32,24,16,512]{3,2,1,0:T(8,128)(2,1)} %hi.3), kind=kLoop, calls=%fused_computation.3 | loop fusion | bytes 2097152 | tf_op jit(solution)/shard_map/squeeze | solution.py:421
  16.6 0.0 collective-permute-done.above
  16.6 1.7 %collective-permute-done.1.below = bf16[24,32,512]{2,1,0:T(8,128)(2,1)} collective-permute-done((bf16[24,32,512]{2,1,0:T(8,128)(2,1)}, bf16[24,32,512]{2,1,0:T(8,128)(2,1)}, u32[]{:S(2)}, u32[]{:S(2)}) %collective-permute-start.1) | collective-permute-done | bytes 786464 | tf_op jit(solution)/shard_map/ppermute | solution.py:18
  18.3 0.8 slice_bitcast_fusion.6
  19.2 0.1 pad_maximum_fusion.1
  19.3 1.3 %collective-permute-start.3 = (bf16[40,16,512]{2,1,0:T(8,128)(2,1)S(1)}, bf16[40,16,512]{2,1,0:T(8,128)(2,1)S(1)}, u32[]{:S(2)}, u32[]{:S(2)}) collective-permute-start(bf16[40,16,512]{2,1,0:T(8,128)(2,1)S(1)} %pad_maximum_fusion.1), channel_id=1, source_target_pairs={{2,0},{4,2},{6,4},{8,6},{10,8},{12,10},{14,12},{3,1},{5,3},{7,5},{... | collective-permute-start | bytes 1966088 | tf_op jit(solution)/shard_map/ppermute | solution.py:18
  20.6 0.1 pad_maximum_fusion
  20.6 4.9 %collective-permute-start.2 = (bf16[40,16,512]{2,1,0:T(8,128)(2,1)S(1)}, bf16[40,16,512]{2,1,0:T(8,128)(2,1)S(1)}, u32[]{:S(2)}, u32[]{:S(2)}) collective-permute-start(bf16[40,16,512]{2,1,0:T(8,128)(2,1)S(1)} %pad_maximum_fusion), channel_id=1, source_target_pairs={{0,2},{2,4},{4,6},{6,8},{8,10},{10,12},{12,14},{1,3},{3,5},{5,7},{... | collective-permute-start | bytes 1966088 | tf_op jit(solution)/shard_map/ppermute | solution.py:18
  25.6 57.4 %inner.1.cost_in = f32[26,24,512]{2,1,0:T(8,128)S(1)} custom-call(bf16[32,24,16,512]{3,2,1,0:T(8,128)(2,1)} %hi.3, bf16[32,24,16,512]{3,2,1,0:T(8,128)(2,1)} %hi.3, bf16[24,32,512]{2,1,0:T(8,128)(2,1)S(1)} %collective-permute-done.above, bf16[24,64,512]{2,1,0:T(8,128)(2,1)S(1)} %get-tuple-element.12.local, ...), custom_call_target="tpu_custom_call" | custom-call | flops 35433480192 | bytes 12582912 | tf_op jit(solution)/shard_map/inner/pallas_call | solution.py:434
  83.1 9.9 %rim.1.cost = f32[26,24,512]{2,1,0:T(8,128)S(1)} custom-call(bf16[32,24,16,512]{3,2,1,0:T(8,128)(2,1)} %hi.3, bf16[32,24,16,512]{3,2,1,0:T(8,128)(2,1)} %hi.3, bf16[40,16,512]{2,1,0:T(8,128)(2,1)S(1)} %collective-permute-done.2.b_lo.b_hi, bf16[40,16,512]{2,1,0:T(8,128)(2,1)S(1)} %collective-permute-done.2.b_lo.b_hi, ...), custom_call_target="tpu_custom_call" | custom-call | flops 3221225472 | bytes 3145728 | tf_op jit(solution)/shard_map/rim/pallas_call | solution.py:464
  93.1 1.1 copy-done
  94.1 20.8 %finish.1 = f32[16,512]{1,0:T(8,128)} custom-call(f32[26,24,512]{2,1,0:T(8,128)} %copy-done), custom_call_target="tpu_custom_call" | custom-call | tf_op jit(solution)/shard_map/finish/pallas_call | solution.py:339
  114.9 1.4 %copy.24 = f32[16,512]{1,0:T(8,128)} copy(f32[16,512]{1,0:T(8,128)} %finish.1) | data formatting | bytes 65536
  (20 shorter events, 0.2 us)
Async XLA Ops:
  0.0 2.1 %copy-start.1 = (bf16[27,32,32]{2,1,0:T(8,128)(2,1)S(1)}, bf16[27,32,32]{2,1,0:T(8,128)(2,1)}, u32[]{:S(2)}) copy-start(bf16[27,32,32]{2,1,0:T(8,128)(2,1)} %param.5) | copy-start | bytes 165892
  2.4 12.7 %copy-start.2 = (f32[32]{0:T(128)S(1)}, f32[32]{0:T(128)}, u32[]{:S(2)}) copy-start(f32[32]{0:T(128)} %param.6) | copy-start | bytes 388
  11.4 5.2 %collective-permute-start = (bf16[24,32,512]{2,1,0:T(8,128)(2,1)}, bf16[24,32,512]{2,1,0:T(8,128)(2,1)S(1)}, u32[]{:S(2)}, u32[]{:S(2)}) collective-permute-start(bf16[24,32,512]{2,1,0:T(8,128)(2,1)} %get-tuple-element.11), channel_id=1, source_target_pairs={{0,1},{2,3},{4,5},{6,7},{8,9},{10,11},{12,13},{14,15},{16,17},{18,... | collective-permute-start | bytes 2359304 | tf_op jit(solution)/shard_map/ppermute | solution.py:18
  13.8 4.5 %collective-permute-start.1 = (bf16[24,32,512]{2,1,0:T(8,128)(2,1)}, bf16[24,32,512]{2,1,0:T(8,128)(2,1)}, u32[]{:S(2)}, u32[]{:S(2)}) collective-permute-start(bf16[24,32,512]{2,1,0:T(8,128)(2,1)} %get-tuple-element.13), channel_id=1, source_target_pairs={{1,0},{3,2},{5,4},{7,6},{9,8},{11,10},{13,12},{15,14},{17,16},{19,... | collective-permute-start | bytes 2359304 | tf_op jit(solution)/shard_map/ppermute | solution.py:18
  19.3 63.8 %collective-permute-start.3 = (bf16[40,16,512]{2,1,0:T(8,128)(2,1)S(1)}, bf16[40,16,512]{2,1,0:T(8,128)(2,1)S(1)}, u32[]{:S(2)}, u32[]{:S(2)}) collective-permute-start(bf16[40,16,512]{2,1,0:T(8,128)(2,1)S(1)} %pad_maximum_fusion.1), channel_id=1, source_target_pairs={{2,0},{4,2},{6,4},{8,6},{10,8},{12,10},{14,12},{3,1},{5,3},{7,5},{... | collective-permute-start | bytes 1966088 | tf_op jit(solution)/shard_map/ppermute | solution.py:18
  20.6 62.3 %collective-permute-start.2 = (bf16[40,16,512]{2,1,0:T(8,128)(2,1)S(1)}, bf16[40,16,512]{2,1,0:T(8,128)(2,1)S(1)}, u32[]{:S(2)}, u32[]{:S(2)}) collective-permute-start(bf16[40,16,512]{2,1,0:T(8,128)(2,1)S(1)} %pad_maximum_fusion), channel_id=1, source_target_pairs={{0,2},{2,4},{4,6},{6,8},{8,10},{10,12},{12,14},{1,3},{3,5},{5,7},{... | collective-permute-start | bytes 1966088 | tf_op jit(solution)/shard_map/ppermute | solution.py:18
  93.1 1.1 copy-start

commit v5 on v4

--- a/solution.py
+++ b/solution.py
@@ -97,7 +97,7 @@
 
 
 def moved(x, step):
-    return move(x.astype(F32), step).astype(BF) if step else x
+    return move(x, step) if step else x
 
 
 def put_half(x3, xe, slot, x, top, bottom):

time: 117 us -> 116 us (level)
  Pallas kernels: 97.1 us -> 95.7 us
where the time goes in v5:
time: 116 us; the launch traced here: 115 us
  Pallas kernels  95.7 us (82%)
  starting transfers between devices  9.92 us (9%)
  local copies, waits for them, and re-layouts  6.86 us (6%)
  waiting for transfers between devices  1.73 us (1%)
    pallas_call x1, Pallas kernels, body(): pl.pallas_call(inner_kernel, grid=(planes,), in_specs=[pl.BlockSpec((ch,...  56.2 us
    pallas_call x1, Pallas kernels, finish(): pl.pallas_call(functools.partial(finish_kernel, planes), in_specs=[pl.Blo...  20.8 us
    ppermute x4, starting transfers between devices, shifted(): return lax.ppermute(x, axis, pairs)  9.92 us
    pallas_call x1, Pallas kernels, body(): pl.pallas_call(functools.partial(rim_kernel, planes), grid=(6,), in_specs...  9.72 us
    pallas_call x1, Pallas kernels, body(): pl.pallas_call(prep_kernel, grid=(planes // group,), in_specs=[pl.BlockSp...  8.98 us
    unnamed x9, local copies, waits for them, and re-layouts  2.59 us
  transfers between devices with their start and end apart: 4, of which 1 were waited for; matrix products, arithmetic and copies ran while one was open for 1% of the time, Pallas kernels for 49%

profile of v5, /device:TPU:0, one launch (start us, length us, event | category | flops | bytes accessed | tf_op | source)
XLA Modules:
  0.0 114.9 jit_solution(13971910907178539616)
XLA Ops:
  0.0 1.0 slice.58
  1.0 0.1 copy.17
  1.1 0.1 reshape.55
  1.3 0.7 tile.6
  2.0 0.1 tile.7.wreg
  2.1 0.3 convolution_bitcast_fusion.wide
  2.4 0.0 copy-start.2
  2.4 9.0 %prep.1 = (bf16[24,32,512]{2,1,0:T(8,128)(2,1)}, bf16[24,32,512]{2,1,0:T(8,128)(2,1)}, bf16[24,64,512]{2,1,0:T(8,128)(2,1)S(1)}, bf16[256,3840]{1,0:T(8,128)(2,1...) custom-call(bf16[32,24,16,512]{3,2,1,0:T(8,128)(2,1)} %hi.3, ...), custom_call_target="tpu_custom_call" | custom-call | flops 1610612736 | bytes 12582912 | tf_op jit(solution)/shard_map/prep/pallas_call | solution.py:381
  11.4 2.4 %collective-permute-start = (bf16[24,32,512]{2,1,0:T(8,128)(2,1)}, bf16[24,32,512]{2,1,0:T(8,128)(2,1)S(1)}, u32[]{:S(2)}, u32[]{:S(2)}) collective-permute-start(bf16[24,32,512]{2,1,0:T(8,128)(2,1)} %get-tuple-element.11), channel_id=1, source_target_pairs={{0,1},{2,3},{4,5},{6,7},{8,9},{10,11},{12,13},{14,15},{16,17},{18,... | collective-permute-start | bytes 2359304 | tf_op jit(solution)/shard_map/ppermute | solution.py:18
  13.8 1.3 %collective-permute-start.1 = (bf16[24,32,512]{2,1,0:T(8,128)(2,1)}, bf16[24,32,512]{2,1,0:T(8,128)(2,1)}, u32[]{:S(2)}, u32[]{:S(2)}) collective-permute-start(bf16[24,32,512]{2,1,0:T(8,128)(2,1)} %get-tuple-element.13), channel_id=1, source_target_pairs={{1,0},{3,2},{5,4},{7,6},{9,8},{11,10},{13,12},{15,14},{17,16},{19,... | collective-permute-start | bytes 2359304 | tf_op jit(solution)/shard_map/ppermute | solution.py:18
  15.1 0.1 broadcast_in_dim_tile.4.bias
  15.3 1.3 %slice_bitcast_fusion = (bf16[32,16,512]{2,1,0:T(8,128)(2,1)S(1)}, bf16[32,16,512]{2,1,0:T(8,128)(2,1)S(1)}) fusion(bf16[32,24,16,512]{3,2,1,0:T(8,128)(2,1)} %hi.3), kind=kLoop, calls=%fused_computation.3 | loop fusion | bytes 2097152 | tf_op jit(solution)/shard_map/squeeze | solution.py:421
  16.6 0.0 collective-permute-done.above
  16.6 1.7 %collective-permute-done.1.below = bf16[24,32,512]{2,1,0:T(8,128)(2,1)} collective-permute-done((bf16[24,32,512]{2,1,0:T(8,128)(2,1)}, bf16[24,32,512]{2,1,0:T(8,128)(2,1)}, u32[]{:S(2)}, u32[]{:S(2)}) %collective-permute-start.1) | collective-permute-done | bytes 786464 | tf_op jit(solution)/shard_map/ppermute | solution.py:18
  18.3 0.8 slice_bitcast_fusion.6
  19.2 0.1 pad_maximum_fusion.1
  19.3 1.3 %collective-permute-start.3 = (bf16[40,16,512]{2,1,0:T(8,128)(2,1)S(1)}, bf16[40,16,512]{2,1,0:T(8,128)(2,1)S(1)}, u32[]{:S(2)}, u32[]{:S(2)}) collective-permute-start(bf16[40,16,512]{2,1,0:T(8,128)(2,1)S(1)} %pad_maximum_fusion.1), channel_id=1, source_target_pairs={{2,0},{4,2},{6,4},{8,6},{10,8},{12,10},{14,12},{3,1},{5,3},{7,5},{... | collective-permute-start | bytes 1966088 | tf_op jit(solution)/shard_map/ppermute | solution.py:18
  20.6 0.1 pad_maximum_fusion
  20.6 4.9 %collective-permute-start.2 = (bf16[40,16,512]{2,1,0:T(8,128)(2,1)S(1)}, bf16[40,16,512]{2,1,0:T(8,128)(2,1)S(1)}, u32[]{:S(2)}, u32[]{:S(2)}) collective-permute-start(bf16[40,16,512]{2,1,0:T(8,128)(2,1)S(1)} %pad_maximum_fusion), channel_id=1, source_target_pairs={{0,2},{2,4},{4,6},{6,8},{8,10},{10,12},{12,14},{1,3},{3,5},{5,7},{... | collective-permute-start | bytes 1966088 | tf_op jit(solution)/shard_map/ppermute | solution.py:18
  25.6 56.2 %inner.1.cost_in = f32[26,24,512]{2,1,0:T(8,128)S(1)} custom-call(bf16[32,24,16,512]{3,2,1,0:T(8,128)(2,1)} %hi.3, bf16[32,24,16,512]{3,2,1,0:T(8,128)(2,1)} %hi.3, bf16[24,32,512]{2,1,0:T(8,128)(2,1)S(1)} %collective-permute-done.above, bf16[24,64,512]{2,1,0:T(8,128)(2,1)S(1)} %get-tuple-element.12.local, ...), custom_call_target="tpu_custom_call" | custom-call | flops 35433480192 | bytes 12582912 | tf_op jit(solution)/shard_map/inner/pallas_call | solution.py:434
  82.0 9.7 %rim.1.cost = f32[26,24,512]{2,1,0:T(8,128)S(1)} custom-call(bf16[32,24,16,512]{3,2,1,0:T(8,128)(2,1)} %hi.3, bf16[32,24,16,512]{3,2,1,0:T(8,128)(2,1)} %hi.3, bf16[40,16,512]{2,1,0:T(8,128)(2,1)S(1)} %collective-permute-done.2.b_lo.b_hi, bf16[40,16,512]{2,1,0:T(8,128)(2,1)S(1)} %collective-permute-done.2.b_lo.b_hi, ...), custom_call_target="tpu_custom_call" | custom-call | flops 3221225472 | bytes 3145728 | tf_op jit(solution)/shard_map/rim/pallas_call | solution.py:464
  91.7 1.1 copy-done
  92.8 20.8 %finish.1 = f32[16,512]{1,0:T(8,128)} custom-call(f32[26,24,512]{2,1,0:T(8,128)} %copy-done), custom_call_target="tpu_custom_call" | custom-call | tf_op jit(solution)/shard_map/finish/pallas_call | solution.py:339
  113.5 1.4 %copy.24 = f32[16,512]{1,0:T(8,128)} copy(f32[16,512]{1,0:T(8,128)} %finish.1) | data formatting | bytes 65536
  (20 shorter events, 0.2 us)
Async XLA Ops:
  0.0 2.1 %copy-start.1 = (bf16[27,32,32]{2,1,0:T(8,128)(2,1)S(1)}, bf16[27,32,32]{2,1,0:T(8,128)(2,1)}, u32[]{:S(2)}) copy-start(bf16[27,32,32]{2,1,0:T(8,128)(2,1)} %param.5) | copy-start | bytes 165892
  2.4 12.7 %copy-start.2 = (f32[32]{0:T(128)S(1)}, f32[32]{0:T(128)}, u32[]{:S(2)}) copy-start(f32[32]{0:T(128)} %param.6) | copy-start | bytes 388
  11.4 5.2 %collective-permute-start = (bf16[24,32,512]{2,1,0:T(8,128)(2,1)}, bf16[24,32,512]{2,1,0:T(8,128)(2,1)S(1)}, u32[]{:S(2)}, u32[]{:S(2)}) collective-permute-start(bf16[24,32,512]{2,1,0:T(8,128)(2,1)} %get-tuple-element.11), channel_id=1, source_target_pairs={{0,1},{2,3},{4,5},{6,7},{8,9},{10,11},{12,13},{14,15},{16,17},{18,... | collective-permute-start | bytes 2359304 | tf_op jit(solution)/shard_map/ppermute | solution.py:18
  13.8 4.5 %collective-permute-start.1 = (bf16[24,32,512]{2,1,0:T(8,128)(2,1)}, bf16[24,32,512]{2,1,0:T(8,128)(2,1)}, u32[]{:S(2)}, u32[]{:S(2)}) collective-permute-start(bf16[24,32,512]{2,1,0:T(8,128)(2,1)} %get-tuple-element.13), channel_id=1, source_target_pairs={{1,0},{3,2},{5,4},{7,6},{9,8},{11,10},{13,12},{15,14},{17,16},{19,... | collective-permute-start | bytes 2359304 | tf_op jit(solution)/shard_map/ppermute | solution.py:18
  19.3 62.7 %collective-permute-start.3 = (bf16[40,16,512]{2,1,0:T(8,128)(2,1)S(1)}, bf16[40,16,512]{2,1,0:T(8,128)(2,1)S(1)}, u32[]{:S(2)}, u32[]{:S(2)}) collective-permute-start(bf16[40,16,512]{2,1,0:T(8,128)(2,1)S(1)} %pad_maximum_fusion.1), channel_id=1, source_target_pairs={{2,0},{4,2},{6,4},{8,6},{10,8},{12,10},{14,12},{3,1},{5,3},{7,5},{... | collective-permute-start | bytes 1966088 | tf_op jit(solution)/shard_map/ppermute | solution.py:18
  20.6 61.2 %collective-permute-start.2 = (bf16[40,16,512]{2,1,0:T(8,128)(2,1)S(1)}, bf16[40,16,512]{2,1,0:T(8,128)(2,1)S(1)}, u32[]{:S(2)}, u32[]{:S(2)}) collective-permute-start(bf16[40,16,512]{2,1,0:T(8,128)(2,1)S(1)} %pad_maximum_fusion), channel_id=1, source_target_pairs={{0,2},{2,4},{4,6},{6,8},{8,10},{10,12},{12,14},{1,3},{3,5},{5,7},{... | collective-permute-start | bytes 1966088 | tf_op jit(solution)/shard_map/ppermute | solution.py:18
  91.7 1.1 copy-start
